TPU v7x, 128 devices: a whole 4x4x4 slice. The times are simulated.
128 devices in a mesh: seq: 128 (over x, y, z, core).
Axes of the slice: x: 4, y: 4, z: 4, core: 2. Of those that a mesh axis runs over, the one named last changes fastest.
Arguments:
- inputs: bfloat16 [2, 32768, 1536], P(None, 'seq'), may hold values from -8 to 8
- ln_gain: float32 [1536], replicated, may hold values from 0.25 to 1.75
- w_in: bfloat16 [1536, 3072], replicated, may hold values from -0.15625 to 0.15625
- kernel: float32 [32, 1536], replicated, may hold values from -1 to 1
- bn_gain: float32 [1536], replicated, may hold values from 0.25 to 1.75
- bn_bias: float32 [1536], replicated, may hold values from -0.6 to 0.6
- w_out: bfloat16 [1536, 1536], replicated, may hold values from -0.15625 to 0.15625
- cotangent: bfloat16 [2, 32768, 1536], P(None, 'seq'), may hold values from -24 to 24
Outputs:
- outputs: bfloat16 [2, 32768, 1536], P(None, 'seq')
- d_inputs: bfloat16 [2, 32768, 1536], P(None, 'seq')
- d_w_out: float32 [1536, 1536], P('seq')
- d_kernel: float32 [32, 1536], replicated
- d_bn_gain: float32 [1536], replicated
- d_bn_bias: float32 [1536], replicated
All inputs are finite; a program needn't handle non-finite values.
Results may differ from a plain program's by a relative error of at most 0.0075.
Values may be sent and summed in bfloat16 or wider, within the bound.
A program may use at most 128 MiB of HBM per device.

v0:
```python
import jax
import jax.numpy as jnp
from jax import lax
from jax.sharding import PartitionSpec as P

D = 1536
K = 32
FRAMES_DEV = 256
UTT = 2


EPSILON = 1e-05


def with_halo(block, sides, width):
    for axis, dim in sides:
        count = lax.axis_size(axis)
        forward = [(i, i + 1) for i in range(count - 1)]
        backward = [(target, source) for source, target in forward]
        low = lax.ppermute(
            lax.slice_in_dim(block, block.shape[dim] - width, None, axis=dim), axis, forward
        )
        high = lax.ppermute(lax.slice_in_dim(block, 0, width, axis=dim), axis, backward)
        block = jnp.concatenate([low, block, high], axis=dim)
    return block


def on_device(inputs, ln_gain, w_in, kernel, bn_gain, bn_bias, w_out, cotangent):
    devices_seq = lax.axis_size("seq")
    frame_total = UTT * FRAMES_DEV * devices_seq
    rows_here = UTT * FRAMES_DEV
    x_float = inputs.astype(jnp.float32)
    ln_mean = jnp.mean(x_float, axis=-1, keepdims=True)
    centred = x_float - ln_mean
    ln_rstd = lax.rsqrt(jnp.mean(centred * centred, axis=-1, keepdims=True) + EPSILON)
    ln_hat = centred * ln_rstd
    normed = (ln_hat * ln_gain).astype(jnp.bfloat16).reshape(rows_here, D)
    proj = jnp.dot(normed, w_in, preferred_element_type=jnp.float32)
    value_half = proj[:, :D]
    gate_sig = jax.nn.sigmoid(proj[:, D:])
    gated = (value_half * gate_sig).astype(jnp.bfloat16).reshape(UTT, FRAMES_DEV, D)
    padded = with_halo(gated, (("seq", 1),), 16)
    conv_out = jnp.zeros((UTT, FRAMES_DEV, D), jnp.float32)
    for tap_index in range(K):
        conv_out = conv_out + kernel[tap_index] * padded[
            :, tap_index + 1 : tap_index + 1 + FRAMES_DEV
        ].astype(jnp.float32)
    bn_mean = lax.psum(jnp.sum(conv_out, axis=(0, 1)), "seq") / frame_total
    deviate = conv_out - bn_mean
    bn_var = lax.psum(jnp.sum(deviate * deviate, axis=(0, 1)), "seq") / frame_total
    bn_rstd = lax.rsqrt(bn_var + EPSILON)
    normed_bn = deviate * bn_rstd
    bn_out = normed_bn * bn_gain + bn_bias
    act_sig = jax.nn.sigmoid(bn_out)
    act = (bn_out * act_sig).astype(jnp.bfloat16).reshape(rows_here, D)
    branch = lax.dot_general(
        act, w_out, (((1,), (1,)), ((), ())), preferred_element_type=jnp.float32
    )
    outputs = (
        (x_float.reshape(rows_here, D) + branch).astype(jnp.bfloat16).reshape(UTT, FRAMES_DEV, D)
    )
    cot_rows = cotangent.reshape(rows_here, D)
    d_w_out = lax.psum_scatter(
        lax.dot_general(
            cot_rows, act, (((0,), (0,)), ((), ())), preferred_element_type=jnp.float32
        ),
        "seq",
        scatter_dimension=0,
        tiled=True,
    )
    d_act = jnp.dot(cot_rows, w_out, preferred_element_type=jnp.float32)
    d_bn = d_act.reshape(UTT, FRAMES_DEV, D) * (act_sig + bn_out * act_sig * (1.0 - act_sig))
    scaled_grad = d_bn * bn_gain
    local_bias = jnp.sum(d_bn, axis=(0, 1))
    local_gain = jnp.sum(d_bn * normed_bn, axis=(0, 1))
    d_bn_bias, d_bn_gain = lax.psum((local_bias, local_gain), "seq")
    mean_grad = bn_gain * d_bn_bias / frame_total
    mean_cross = bn_gain * d_bn_gain / frame_total
    d_conv = bn_rstd * (scaled_grad - mean_grad - normed_bn * mean_cross)
    kernel_rows = []
    for tap_index in range(K):
        window = padded[:, tap_index + 1 : tap_index + 1 + FRAMES_DEV].astype(jnp.float32)
        kernel_rows.append(jnp.sum(window * d_conv, axis=(0, 1)))
    d_kernel = lax.psum(jnp.stack(kernel_rows), "seq")
    grad_padded = with_halo(d_conv.astype(jnp.bfloat16), (("seq", 1),), 16).astype(d_conv.dtype)
    d_gated = jnp.zeros((UTT, FRAMES_DEV, D), jnp.float32)
    for tap_index in range(K):
        d_gated = (
            d_gated
            + kernel[tap_index] * grad_padded[:, 31 - tap_index : 31 - tap_index + FRAMES_DEV]
        )
    d_gated = d_gated.reshape(rows_here, D)
    d_value = d_gated * gate_sig
    d_gate = d_gated * value_half * gate_sig * (1.0 - gate_sig)
    d_proj = jnp.concatenate([d_value, d_gate], axis=-1).astype(jnp.bfloat16)
    d_normed = lax.dot_general(
        d_proj, w_in, (((1,), (1,)), ((), ())), preferred_element_type=jnp.float32
    )
    d_hat = d_normed.reshape(UTT, FRAMES_DEV, D) * ln_gain
    d_layer = ln_rstd * (
        d_hat
        - jnp.mean(d_hat, axis=-1, keepdims=True)
        - ln_hat * jnp.mean(d_hat * ln_hat, axis=-1, keepdims=True)
    )
    d_inputs = (cotangent.astype(jnp.float32) + d_layer).astype(jnp.bfloat16)
    return (outputs, d_inputs, d_w_out, d_kernel, d_bn_gain, d_bn_bias)


def solution(mesh):
    return jax.shard_map(
        on_device,
        mesh=mesh,
        in_specs=(P(None, "seq", None), P(), P(), P(), P(), P(), P(), P(None, "seq", None)),
        out_specs=(P(None, "seq", None), P(None, "seq", None), P("seq", None), P(), P(), P()),
        check_vma=False,
    )
```

profile of v0, /device:TPU:1, one launch (start us, length us, event | category | flops | bytes accessed | tf_op | source)
XLA Modules:
  0.0 475.8 jit_solution(6670448868981798242)
XLA Ops:
  7.2 0.0 all-reduce.5.cloned.1.call-start
  7.2 1.8 convert_reduce_fusion
  9.1 2.0 multiply_reduce_fusion.4
  11.0 0.5 multiply_convert_fusion.1
  11.6 0.0 copy-done.55
  11.6 7.6 %fusion.148 = f32[512,3072]{1,0:T(8,128)S(1)} fusion(bf16[512,1536]{1,0:T(8,128)(2,1)S(1)} %bitcast.51, bf16[1536,3072]{1,0:T(8,128)(2,1)} %param.10), kind=kOutput, calls=%fused_computation.333 | convolution fusion | flops 4831838208 | bytes 17301504 | tf_op jit(solution)/shard_map/dot_general | solution.py:38
  19.2 0.0 copy-start.7
  19.2 0.8 multiply_convert_fusion
  20.1 1.7 copy-done
  21.8 0.7 fusion.147
  22.5 3.3 collective-permute-start.1
  25.8 3.6 collective-permute-start
  29.3 0.9 slice_reduce_fusion.31
  30.3 0.2 slice_reduce_fusion.30
  30.6 0.7 collective-permute-done
  31.3 17.2 %fusion.144 = (f32[1536]{0:T(1024)S(1)}, f32[2,256,1536]{2,1,0:T(8,128)}) fusion(bf16[2,16,1536]{2,1,0:T(8,128)(2,1)S(1)} %collective-permute-done.1, bf16[2,256,1536]{2,1,0:T(8,128)(2,1)S(1)} %bitcast.42, f32[1536]{0:T(1024)S(1)} %get-tuple-element.82, f32[1536]{0:T(1024)S(1)} %get-tuple-element.83, f32[1536]{0:T(1024)S(1)} %get-tuple-element.53, ...), kind=kLoop, calls=%fused_computation.330 | loop fusion | flops 148634112 | bytes 5117952 | tf_op jit(solution)/shard_map/reduce_sum | solution.py:48
  48.5 73.1 %psum.35 = f32[1536]{0:T(1024)S(1)} all-reduce(f32[1536]{0:T(1024)S(1)} %get-tuple-element.89), channel_id=1, replica_groups=mesh['seq'=128] {'seq'}, use_global_device_ids=true, to_apply=%region_3.0 | all-reduce | flops 1536 | bytes 12288 | tf_op jit(solution)/shard_map/psum | solution.py:48
  121.6 2.2 multiply_reduce_fusion.3
  123.8 64.1 %psum.36 = f32[1536]{0:T(1024)S(1)} all-reduce(f32[1536]{0:T(1024)S(1)} %multiply_reduce_fusion.3), channel_id=1, replica_groups=mesh['seq'=128] {'seq'}, use_global_device_ids=true, to_apply=%region_5.0 | all-reduce | flops 1536 | bytes 12288 | tf_op jit(solution)/shard_map/psum | solution.py:50
  188.0 9.6 %fusion.143 = (f32[1536]{0:T(1024)S(1)}, f32[1536]{0:T(1024)S(1)}, bf16[2,256,1536]{2,1,0:T(8,128)(2,1)}, f32[2,256,1536]{2,1,0:T(8,128)}) fusion(f32[1536]{0:T(1024)S(1)} %add_rsqrt_fusion, f32[2,256,1536]{2,1,0:T(8,128)} %get-tuple-element.90, f32[1536]{0:T(1024)S(1)} %broadcast_multiply_fusion, f32[1536]{0:T(1024)S(1)} %copy-done.60, ...), kind=kOutput, calls=%fused_computation.329 | convolution fusion | flops 2428498944 | bytes 14192640 | tf_op jit(solution)/shard_map/dot_general | solution.py:71
  197.6 63.0 %all-reduce.1 = (f32[1536]{0:T(1024)S(1)}, f32[1536]{0:T(1024)S(1)}) all-reduce(f32[1536]{0:T(1024)S(1)} %get-tuple-element.51, f32[1536]{0:T(1024)S(1)} %get-tuple-element.50), channel_id=1, replica_groups=mesh['seq'=128] {'seq'}, use_global_device_ids=true, to_apply=%region_9.0 | all-reduce | flops 3072 | bytes 24576 | tf_op jit(solution)/shard_map/psum | solution.py:76
  260.6 0.0 slice-start.2
  260.6 8.1 %fusion.67 = (f32[1536]{0:T(1024)S(1)}, f32[1536]{0:T(1024)S(1)}, f32[1536]{0:T(1024)S(1)}, f32[1536]{0:T(1024)S(1)}, f32[1536]{0:T(1024)S(1)}, /*index=5*/f32[1...) fusion(bf16[2,16,1536]{2,1,0:T(8,128)(2,1)S(1)} %collective-permute-done.1, ...), kind=kLoop, calls=%fused_computation.160 | loop fusion | flops 47958528 | bytes 11194368 | tf_op jit(solution)/shard_map/reduce_sum | solution.py:83
  268.8 0.0 slice-start.3
  268.8 0.0 copy-start.61
  268.8 7.1 %fusion.52 = (f32[1536]{0:T(1024)S(1)}, f32[1536]{0:T(1024)S(1)}, f32[1536]{0:T(1024)S(1)}, f32[1536]{0:T(1024)S(1)}, f32[1536]{0:T(1024)S(1)}, /*index=5*/f32[1...) fusion(f32[2,256,1536]{2,1,0:T(8,128)S(1)} %get-tuple-element.88, ...), kind=kLoop, calls=%fused_computation.145 | loop fusion | flops 40095744 | bytes 12730368 | tf_op jit(solution)/shard_map/reduce_sum | solution.py:83
  275.9 2.5 collective-permute-start.3
  278.4 3.1 collective-permute-start.2
  281.5 3.8 fusion.110
  285.3 2.8 fusion.35
  288.1 0.0 copy-start.5
  288.1 4.1 fusion.44
  292.2 5.1 %convolution_bitcast_fusion = f32[1536,1536]{0,1:T(8,128)} fusion(bf16[2,256,1536]{2,1,0:T(8,128)(2,1)S(1)} %copy-done.61, bf16[2,256,1536]{2,1,0:T(8,128)(2,1)S(1)} %copy-done.5), kind=kOutput, calls=%fused_computation.29 | convolution fusion | flops 2415919104 | bytes 12582912 | tf_op jit(solution)/shard_map/dot_general | solution.py:64
  297.7 2.8 stack.131
  300.5 0.0 all-reduce.5.cloned.1.call-update
  300.9 1.1 copy-done.4
  301.9 1.5 maximum_convert_fusion
  303.7 12.4 %fusion.68 = f32[2,256,1536]{2,1,0:T(8,128)S(1)} fusion(f32[2,288,1536]{2,1,0:T(8,128)S(1)} %maximum_convert_fusion, f32[1536]{0:T(1024)S(1)} %copy-done.48, f32[1536]{0:T(1024)S(1)} %copy-done.50, f32[1536]{0:T(1024)S(1)} %get-tuple-element.53, f32[1536]{0:T(1024)S(1)} %copy-done.8, f32[1536]{0:T(1024)S(1)} %copy-done.9, f32[1536]{0:T(1024)S(1)} %copy-done.10, ...), kind=kLoop, calls=%fused_computation.162 | loop fusion | flops 49545216 | bytes 104005632 | tf_op jit(solution)/shard_map/add | solution.py:89
  316.2 0.0 copy-start.52
  316.2 1.6 fusion.106
  317.8 9.2 %multiply_reduce_fusion.1 = (f32[512]{0:T(512)S(1)}, f32[512,1536]{1,0:T(8,128)}) fusion(f32[1536]{0:T(1024)S(1)} %copy-done.52, bf16[1536,3072]{1,0:T(8,128)(2,1)} %param.10, bf16[512,1536]{1,0:T(8,128)(2,1)S(1)} %get-tuple-element.92, bf16[512,1536]{1,0:T(8,128)(2,1)S(1)} %get-tuple-element.91), kind=kOutput, calls=%fused_computation.240 | convolution fusion | flops 4839702016 | bytes 15736832 | tf_op jit(solution)/shard_map/dot_general | solution.py:96
  327.1 2.9 multiply_reduce_fusion
  330.0 0.6 copy-done.2
  330.6 2.4 add_convert_fusion
  333.1 131.7 %all-reduce.5.cloned.1.call-done = (f32[1536,1536]{0,1:T(8,128)}, f32[32,1536]{1,0:T(8,128)}) async-done(((f32[1536,1536]{0,1:T(8,128)}, f32[32,1536]{1,0:T(8,128)}), (f32[1536,1536]{0,1:T(8,128)}, f32[32,1536]{1,0:T(8,128)})) %all-reduce.5.cloned.1.call-update) | async-done | bytes 9633808
  464.7 1.7 constant_dynamic-slice_fusion
  466.4 0.9 copy.17
  467.3 1.6 copy.23
  (168 shorter events, 0.5 us)
Async XLA Ops:
  7.2 3.9 copy-start.1
  7.2 3.9 copy-start.51
  7.2 457.6 %all-reduce.5.cloned.1.call-start = ((), (), s32[]{:S(2)}) async-start(), calls=%async_computation | async-start | bytes 19267584
  19.2 10.1 %copy-start.7 = (f32[32,1536]{1,0:T(8,128)S(1)}, f32[32,1536]{1,0:T(8,128)}, u32[]{:S(2)}) copy-start(f32[32,1536]{1,0:T(8,128)} %param.11) | copy-start | bytes 589828
  22.5 8.1 %collective-permute-start.1 = (bf16[2,16,1536]{2,1,0:T(8,128)(2,1)}, bf16[2,16,1536]{2,1,0:T(8,128)(2,1)S(1)}, u32[]{:S(2)}, u32[]{:S(2)}) collective-permute-start(bf16[2,16,1536]{2,1,0:T(8,128)(2,1)} %get-tuple-element.98), channel_id=1, source_target_pairs={{1,0},{2,1},{3,2},{4,3},{5,4},{6,5},{7,6},{8,7},{9,8},{10,9},{11,1... | collective-permute-start | bytes 294920 | tf_op jit(solution)/shard_map/ppermute | solution.py:23
  25.8 5.5 %collective-permute-start = (bf16[2,16,1536]{2,1,0:T(8,128)(2,1)}, bf16[2,16,1536]{2,1,0:T(8,128)(2,1)S(1)}, u32[]{:S(2)}, u32[]{:S(2)}) collective-permute-start(bf16[2,16,1536]{2,1,0:T(8,128)(2,1)} %get-tuple-element.97), channel_id=1, source_target_pairs={{0,1},{1,2},{2,3},{3,4},{4,5},{5,6},{6,7},{7,8},{8,9},{9,10},{10,1... | collective-permute-start | bytes 294920 | tf_op jit(solution)/shard_map/ppermute | solution.py:20
  30.5 17.9 %copy-start.27 = (f32[1536]{0:T(1024)}, f32[1536]{0:T(1024)S(1)}, u32[]{:S(2)}) copy-start(f32[1536]{0:T(1024)S(1)} %get-tuple-element.72) | copy-start | bytes 18436
  30.5 17.9 %copy-start.29 = (f32[1536]{0:T(1024)}, f32[1536]{0:T(1024)S(1)}, u32[]{:S(2)}) copy-start(f32[1536]{0:T(1024)S(1)} %get-tuple-element.73) | copy-start | bytes 18436
  30.5 17.9 %copy-start.31 = (f32[1536]{0:T(1024)}, f32[1536]{0:T(1024)S(1)}, u32[]{:S(2)}) copy-start(f32[1536]{0:T(1024)S(1)} %get-tuple-element.74) | copy-start | bytes 18436
  30.5 17.9 %copy-start.33 = (f32[1536]{0:T(1024)}, f32[1536]{0:T(1024)S(1)}, u32[]{:S(2)}) copy-start(f32[1536]{0:T(1024)S(1)} %get-tuple-element.75) | copy-start | bytes 18436
  30.5 17.9 %copy-start.35 = (f32[1536]{0:T(1024)}, f32[1536]{0:T(1024)S(1)}, u32[]{:S(2)}) copy-start(f32[1536]{0:T(1024)S(1)} %get-tuple-element.76) | copy-start | bytes 18436
  30.5 17.9 %copy-start.37 = (f32[1536]{0:T(1024)}, f32[1536]{0:T(1024)S(1)}, u32[]{:S(2)}) copy-start(f32[1536]{0:T(1024)S(1)} %get-tuple-element.77) | copy-start | bytes 18436
  30.5 17.9 %copy-start.39 = (f32[1536]{0:T(1024)}, f32[1536]{0:T(1024)S(1)}, u32[]{:S(2)}) copy-start(f32[1536]{0:T(1024)S(1)} %get-tuple-element.78) | copy-start | bytes 18436
  30.6 17.9 %copy-start.41 = (f32[1536]{0:T(1024)}, f32[1536]{0:T(1024)S(1)}, u32[]{:S(2)}) copy-start(f32[1536]{0:T(1024)S(1)} %get-tuple-element.79) | copy-start | bytes 18436
  30.6 17.9 %copy-start.43 = (f32[1536]{0:T(1024)}, f32[1536]{0:T(1024)S(1)}, u32[]{:S(2)}) copy-start(f32[1536]{0:T(1024)S(1)} %get-tuple-element.80) | copy-start | bytes 18436
  30.6 17.9 %copy-start.45 = (f32[1536]{0:T(1024)}, f32[1536]{0:T(1024)S(1)}, u32[]{:S(2)}) copy-start(f32[1536]{0:T(1024)S(1)} %get-tuple-element.81) | copy-start | bytes 18436
  30.6 17.9 %copy-start.47 = (f32[1536]{0:T(1024)}, f32[1536]{0:T(1024)S(1)}, u32[]{:S(2)}) copy-start(f32[1536]{0:T(1024)S(1)} %get-tuple-element.82) | copy-start | bytes 18436
  30.6 17.9 %copy-start.49 = (f32[1536]{0:T(1024)}, f32[1536]{0:T(1024)S(1)}, u32[]{:S(2)}) copy-start(f32[1536]{0:T(1024)S(1)} %get-tuple-element.83) | copy-start | bytes 18436
  31.3 156.7 %copy-start.57 = (f32[1536]{0:T(1024)S(1)}, f32[1536]{0:T(1024)}, u32[]{:S(2)}) copy-start(f32[1536]{0:T(1024)} %param.12) | copy-start | bytes 18436
  31.3 156.7 %copy-start.60 = (f32[1536]{0:T(1024)S(1)}, f32[1536]{0:T(1024)}, u32[]{:S(2)}) copy-start(f32[1536]{0:T(1024)} %param.13) | copy-start | bytes 18436
  260.6 8.2 %copy-start.58 = (f32[1536]{0:T(1024)}, f32[1536]{0:T(1024)S(1)}, u32[]{:S(2)}) copy-start(f32[1536]{0:T(1024)S(1)} %get-tuple-element.108) | copy-start | bytes 18436
  260.6 8.2 %copy-start.59 = (f32[1536]{0:T(1024)}, f32[1536]{0:T(1024)S(1)}, u32[]{:S(2)}) copy-start(f32[1536]{0:T(1024)S(1)} %get-tuple-element.109) | copy-start | bytes 18436
  260.6 20.9 %slice-start.2 = ((s8[4718592]{0:T(1024)(128)(4,1)}), s8[4194304]{0:T(1024)(128)(4,1)S(1)}, s32[]{:S(2)}) async-start(s8[4718592]{0:T(1024)(128)(4,1)} %bitcast.52), calls=%async_computation.3 | async-start | bytes 8388608
  268.8 12.7 %slice-start.3 = ((s8[4718592]{0:T(1024)(128)(4,1)}), s8[524288]{0:T(1024)(128)(4,1)S(1)}, s32[]{:S(2)}) async-start(s8[4718592]{0:T(1024)(128)(4,1)} %bitcast.52), calls=%async_computation.4 | async-start | bytes 1048576
  268.8 12.7 %copy-start.61 = (bf16[2,256,1536]{2,1,0:T(8,128)(2,1)S(1)}, bf16[2,256,1536]{2,1,0:T(8,128)(2,1)}, u32[]{:S(2)}) copy-start(bf16[2,256,1536]{2,1,0:T(8,128)(2,1)} %get-tuple-element.93) | copy-start | bytes 4718596
  275.9 9.4 %copy-start.3 = (bf16[2,256,1536]{2,1,0:T(8,128)(2,1)}, bf16[2,256,1536]{2,1,0:T(8,128)(2,1)S(1)}, u32[]{:S(2)}) copy-start(bf16[2,256,1536]{2,1,0:T(8,128)(2,1)S(1)} %get-tuple-element.94) | copy-start | bytes 4718596
  275.9 24.9 %collective-permute-start.3 = (bf16[2,16,1536]{2,1,0:T(8,128)(2,1)S(1)}, bf16[2,16,1536]{2,1,0:T(8,128)(2,1)S(1)}, u32[]{:S(2)}, u32[]{:S(2)}) collective-permute-start(bf16[2,16,1536]{2,1,0:T(8,128)(2,1)S(1)} %get-tuple-element.96), channel_id=1, source_target_pairs={{1,0},{2,1},{3,2},{4,3},{5,4},{6,5},{7,6},{8,7},{9,8},{10,9},{11,1... | collective-permute-start | bytes 294920 | tf_op jit(solution)/shard_map/ppermute | solution.py:23
  278.4 22.4 %collective-permute-start.2 = (bf16[2,16,1536]{2,1,0:T(8,128)(2,1)S(1)}, bf16[2,16,1536]{2,1,0:T(8,128)(2,1)}, u32[]{:S(2)}, u32[]{:S(2)}) collective-permute-start(bf16[2,16,1536]{2,1,0:T(8,128)(2,1)S(1)} %get-tuple-element.95), channel_id=1, source_target_pairs={{0,1},{1,2},{2,3},{3,4},{4,5},{5,6},{6,7},{7,8},{8,9},{9,10},{10,1... | collective-permute-start | bytes 294920 | tf_op jit(solution)/shard_map/ppermute | solution.py:20
  288.1 4.1 copy-start.5
  300.5 2.9 copy-start.8
  300.5 2.9 copy-start.9
  300.5 2.9 copy-start.10
  300.6 2.9 copy-start.11
  300.6 2.9 copy-start.12
  300.6 2.9 copy-start.13
  300.6 2.9 copy-start.14
  300.6 2.9 copy-start.15
  300.6 2.9 copy-start.16
  300.6 2.9 copy-start.17
  300.6 2.9 copy-start.18
  300.6 2.9 copy-start.19
  300.6 2.9 copy-start.20
  301.9 14.2 %slice-start = ((s8[6291456]{0:T(1024)(128)(4,1)}), s8[4194304]{0:T(1024)(128)(4,1)S(1)}, s32[]{:S(2)}) async-start(s8[6291456]{0:T(1024)(128)(4,1)} %bitcast.47), calls=%async_computation.1 | async-start | bytes 8388608
  303.7 12.4 %slice-start.1 = ((s8[6291456]{0:T(1024)(128)(4,1)}), s8[2097152]{0:T(1024)(128)(4,1)S(1)}, s32[]{:S(2)}) async-start(s8[6291456]{0:T(1024)(128)(4,1)} %bitcast.47), calls=%async_computation.2 | async-start | bytes 4194304
  317.8 9.3 %copy-start.54 = (f32[2,256]{1,0:T(2,128)S(1)}, f32[2,256]{1,0:T(2,128)}, u32[]{:S(2)}) copy-start(f32[2,256]{1,0:T(2,128)} %copy-done.53) | copy-start | bytes 6148
  317.8 9.3 %copy-start.56 = (f32[2,256]{1,0:T(2,128)S(1)}, f32[2,256]{1,0:T(2,128)}, u32[]{:S(2)}) copy-start(f32[2,256]{1,0:T(2,128)} %copy-done.55) | copy-start | bytes 6148
  327.0 3.0 copy-start.6
  327.0 3.6 copy-start.2
  (23 other events, 58.8 us)
Sparse Core Ops, SparseCore 0:
  300.6 164.0 all-reduce.4
where the time goes:
time: 477 us; the launch traced here: 476 us
  blocking collectives  200 us (42%)
  waiting for transfers between devices  132 us (28%)
  other arithmetic  67.4 us (14%)
  matrix products  35.3 us (7%)
  between operations  15.4 us (3%)
  local copies, waits for them, and re-layouts  12.7 us (3%)
  starting transfers between devices  12.4 us (3%)
    unnamed x2, waiting for transfers between devices  132 us
    psum x1, blocking collectives, on_device(): bn_mean = lax.psum(jnp.sum(conv_out, axis=(0, 1)), 'seq') / frame_total  73.1 us
    psum x1, blocking collectives, on_device(): lax.psum(jnp.sum(deviate * deviate, axis=(0, 1)), 'seq') / frame_total  64.1 us
    psum x1, blocking collectives, on_device(): d_bn_bias, d_bn_gain = lax.psum((local_bias, local_gain), 'seq')  63 us
    reduce_sum x4, other arithmetic, on_device(): kernel_rows.append(jnp.sum(window * d_conv, axis=(0, 1)))  22 us
    reduce_sum x1, other arithmetic, on_device(): bn_mean = lax.psum(jnp.sum(conv_out, axis=(0, 1)), 'seq') / frame_total  17.2 us
    add x1, other arithmetic, on_device(): d_gated + kernel[tap_index] * grad_padded[:, 31 - tap_index:31 - tap_inde...  12.4 us
    dot_general x1, matrix products, on_device(): d_act = jnp.dot(cot_rows, w_out, preferred_element_type=jnp.float32)  9.63 us
  transfers between devices with their start and end apart: 5, of which 2 were waited for; matrix products, arithmetic and copies ran while one was open for 10% of the time, Pallas kernels for 0%

commit v1 on v0

--- a/solution.py
+++ b/solution.py
@@ -1,15 +1,376 @@
+import functools
 import jax
 import jax.numpy as jnp
 from jax import lax
+from jax.experimental import pallas as pl
+from jax.experimental.pallas import tpu as pltpu
 from jax.sharding import PartitionSpec as P
 
 D = 1536
 K = 32
 FRAMES_DEV = 256
 UTT = 2
-
-
 EPSILON = 1e-05
+F32 = jnp.float32
+BF16 = jnp.bfloat16
+STRIDE = {"core": 1, "z": 2, "y": 8, "x": 32}
+SIZE = {"core": 2, "z": 4, "y": 4, "x": 4}
+ORDERS = (("x", "y", "z"), ("y", "z", "x"), ("z", "x", "y"))
+HALF = D // 2
+
+
+def coord(me, axis):
+    return lax.rem(me // STRIDE[axis], SIZE[axis])
+
+
+def peers(me, axis):
+    q = coord(me, axis)
+    found = []
+    for delta in range(1, SIZE[axis]):
+        other = lax.rem(q + delta, SIZE[axis])
+        found.append((other, me + (other - q) * STRIDE[axis]))
+    return found
+
+
+class Net:
+    def __init__(self, me, send_sem, recv_sem):
+        self.me, self.send_sem, self.recv_sem, self.used = me, send_sem, recv_sem, 0
+        self.started = []
+
+    def send(self, src, dst, device):
+        slot = self.used
+        self.used += 1
+        copy = pltpu.make_async_remote_copy(
+            src_ref=src,
+            dst_ref=dst,
+            send_sem=self.send_sem.at[slot],
+            recv_sem=self.recv_sem.at[slot],
+            device_id=(device,),
+            device_id_type=pl.DeviceIdType.MESH,
+        )
+        copy.start()
+        self.started.append(copy)
+        return copy
+
+    def drain(self):
+        for copy in self.started:
+            copy.wait_send()
+
+
+def greet(me, axes, extra=()):
+    barrier = pltpu.get_barrier_semaphore()
+    count = 0
+    for axis in axes:
+        for _, device in peers(me, axis):
+            pl.semaphore_signal(
+                barrier, inc=1, device_id=(device,), device_id_type=pl.DeviceIdType.MESH
+            )
+            count += 1
+    for device in extra:
+        pl.semaphore_signal(
+            barrier, inc=1, device_id=(device,), device_id_type=pl.DeviceIdType.MESH
+        )
+        count += 1
+    pl.semaphore_wait(barrier, count)
+
+
+AXES = ("core", "z", "y", "x")
+
+
+def merge_stats(parts, rows):
+    mean = functools.reduce(jnp.add, [p[0:1] for p in parts]) * (1.0 / len(parts))
+    spread = functools.reduce(jnp.add, [p[1:2] for p in parts])
+    for p in parts:
+        gap = p[0:1] - mean
+        spread = spread + rows * gap * gap
+    return jnp.concatenate([mean, spread], axis=0)
+
+
+def reduce_kernel(merge, x_ref, o_ref, cur, got, send_sem, recv_sem):
+    me = lax.axis_index("seq")
+    greet(me, AXES)
+    net = Net(me, send_sem, recv_sem)
+    value = x_ref[...]
+    rows = UTT * FRAMES_DEV
+    slot = 0
+    for level, axis in enumerate(AXES):
+        cur[level] = value
+        copies = []
+        for _, device in peers(me, axis):
+            copies.append((net.send(cur.at[level], got.at[slot], device), slot))
+            slot += 1
+        parts = [value]
+        for copy, index in copies:
+            copy.wait_recv()
+            parts.append(got[index])
+        if merge:
+            value = merge_stats(parts, float(rows))
+        else:
+            value = functools.reduce(jnp.add, parts)
+        rows *= SIZE[axis]
+    o_ref[...] = value
+    net.drain()
+
+
+def reduce_small(x, merge, collective_id):
+    return pl.pallas_call(
+        functools.partial(reduce_kernel, merge),
+        out_shape=jax.ShapeDtypeStruct((2, D), F32),
+        in_specs=[pl.BlockSpec(memory_space=pltpu.VMEM)],
+        out_specs=pl.BlockSpec(memory_space=pltpu.VMEM),
+        scratch_shapes=[
+            pltpu.VMEM((4, 2, D), F32),
+            pltpu.VMEM((10, 2, D), F32),
+            pltpu.SemaphoreType.DMA((10,)),
+            pltpu.SemaphoreType.DMA((10,)),
+        ],
+        compiler_params=pltpu.CompilerParams(collective_id=collective_id, has_side_effects=True),
+    )(x)
+
+
+class DKernel:
+    def __init__(self, net, src, core_buf, got_core, got_x, cz, got_z, cy, got_y, full, other):
+        self.net = net
+        self.src, self.core_buf, self.got_core = src, core_buf, got_core
+        self.got_x, self.cz, self.got_z = got_x, cz, got_z
+        self.cy, self.got_y, self.full, self.other = cy, got_y, full, other
+
+    def start(self):
+        me = self.net.me
+        core = coord(me, "core")
+        self.c0 = [self.net.send(self.src.at[1 - core], self.got_core, me + 1 - 2 * core)]
+
+    def to_x(self):
+        me = self.net.me
+        core = coord(me, "core")
+        x = coord(me, "x")
+        self.c0[0].wait_recv()
+        self.core_buf[...] = self.src[core] + self.got_core[...]
+        self.cx_c = [
+            self.net.send(self.core_buf.at[other], self.got_x.at[i], device)
+            for i, (other, device) in enumerate(peers(me, "x"))
+        ]
+
+    def to_z(self):
+        me = self.net.me
+        total = self.core_buf[coord(me, "x")]
+        for i, copy in enumerate(self.cx_c):
+            copy.wait_recv()
+            total = total + self.got_x[i]
+        self.cz[...] = total
+        self.cz_c = [
+            self.net.send(self.cz, self.got_z.at[i], device)
+            for i, (_, device) in enumerate(peers(me, "z"))
+        ]
+
+    def to_y(self):
+        me = self.net.me
+        total = self.cz[...]
+        for i, copy in enumerate(self.cz_c):
+            copy.wait_recv()
+            total = total + self.got_z[i]
+        self.cy[...] = total
+        self.cy_c = [
+            self.net.send(self.cy, self.got_y.at[i], device)
+            for i, (_, device) in enumerate(peers(me, "y"))
+        ]
+
+    def gather_x(self):
+        me = self.net.me
+        total = self.cy[...]
+        for i, copy in enumerate(self.cy_c):
+            copy.wait_recv()
+            total = total + self.got_y[i]
+        x = coord(me, "x")
+        self.full[x] = total
+        self.gx_c = [
+            self.net.send(self.full.at[x], self.full.at[x], device)
+            for _, device in peers(me, "x")
+        ]
+
+    def gather_core(self):
+        me = self.net.me
+        core = coord(me, "core")
+        for copy in self.gx_c:
+            copy.wait_recv()
+        self.gc_c = self.net.send(self.full, self.other, me + 1 - 2 * core)
+
+    def finish(self, out):
+        core = coord(self.net.me, "core")
+        self.gc_c.wait_recv()
+        for i in range(4):
+            mine = self.full[i]
+            theirs = self.other[i]
+            out[pl.ds(8 * i, 8), 0:HALF] = jnp.where(core == 0, mine, theirs)
+            out[pl.ds(8 * i, 8), HALF:D] = jnp.where(core == 0, theirs, mine)
+
+
+DK_SCRATCH = [
+    pltpu.VMEM((4, 8, HALF), F32),
+    pltpu.VMEM((4, 8, HALF), F32),
+    pltpu.VMEM((3, 8, HALF), F32),
+    pltpu.VMEM((8, HALF), F32),
+    pltpu.VMEM((3, 8, HALF), F32),
+    pltpu.VMEM((8, HALF), F32),
+    pltpu.VMEM((3, 8, HALF), F32),
+    pltpu.VMEM((4, 8, HALF), F32),
+    pltpu.VMEM((4, 8, HALF), F32),
+]
+
+
+def pick(ref, dims, axis, index):
+    where = dims.index(axis)
+    if where == 0:
+        return ref.at[index]
+    if where == 1:
+        return ref.at[:, index]
+    return ref.at[:, :, index]
+
+
+class Scatter:
+    def __init__(self, net, src, got_core, s1, got1, s2, got2, s3, got3, tail, got_tail):
+        self.net, self.src, self.got_core = net, src, got_core
+        self.s = [s1, s2, s3]
+        self.got = [got1, got2, got3]
+        self.tail, self.got_tail = tail, got_tail
+
+    def start(self, part):
+        me = self.net.me
+        core = coord(me, "core")
+        return self.net.send(self.src.at[1 - core, part], self.got_core.at[part], me + 1 - 2 * core)
+
+    def dims(self, part, level):
+        gone = ORDERS[part][:level]
+        return [a for a in ("x", "y", "z") if a not in gone]
+
+    def add_core(self, part, copy):
+        core = coord(self.net.me, "core")
+        copy.wait_recv()
+
+        def body(i, carry):
+            x, y = i // 4, lax.rem(i, 4)
+            mine = self.src[core, part, x, y].astype(F32)
+            theirs = self.got_core[part, x, y].astype(F32)
+            self.s[0][part, x, y] = (mine + theirs).astype(BF16)
+            return carry
+
+        lax.fori_loop(0, 16, body, 0)
+
+    def send_level(self, part, level):
+        me = self.net.me
+        axis = ORDERS[part][level]
+        dims = self.dims(part, level)
+        return [
+            self.net.send(
+                pick(self.s[level].at[part], dims, axis, other),
+                self.got[level].at[part, i],
+                device,
+            )
+            for i, (other, device) in enumerate(peers(me, axis))
+        ]
+
+    def add_level(self, part, level, copies):
+        me = self.net.me
+        axis = ORDERS[part][level]
+        dims = self.dims(part, level)
+        own = pick(self.s[level].at[part], dims, axis, coord(me, axis))
+        for copy in copies:
+            copy.wait_recv()
+        got = self.got[level].at[part]
+        if level == 2:
+            total = own[...].astype(F32)
+            for i in range(3):
+                total = total + got[i].astype(F32)
+            return total
+        for a in range(4):
+            total = own[a].astype(F32)
+            for i in range(3):
+                total = total + got[i, a].astype(F32)
+            self.s[level + 1][part, a] = total.astype(BF16)
+
+    def exchange(self, totals):
+        core = coord(self.net.me, "core")
+        self.mine = []
+        for part in range(3):
+            for half in range(2):
+                low = totals[part][half * 24 : half * 24 + 12]
+                high = totals[part][half * 24 + 12 : half * 24 + 24]
+                self.mine.append(jnp.where(core == 0, low, high))
+                self.tail[part * 2 + half] = jnp.where(core == 0, high, low)
+        self.copy = self.net.send(self.tail, self.got_tail, self.net.me + 1 - 2 * core)
+
+    def finish(self, out):
+        core = coord(self.net.me, "core")
+        self.copy.wait_recv()
+        for piece in range(6):
+            mine = self.mine[piece]
+            theirs = self.got_tail[piece]
+            out[:, piece * 128 : piece * 128 + 128] = jnp.where(core == 0, mine, theirs)
+            out[:, HALF + piece * 128 : HALF + piece * 128 + 128] = jnp.where(core == 0, theirs, mine)
+
+
+RS_SCRATCH = [
+    pltpu.VMEM((3, 4, 4, 4, 48, 128), BF16),
+    pltpu.VMEM((3, 4, 4, 4, 48, 128), BF16),
+    pltpu.VMEM((3, 3, 4, 4, 48, 128), BF16),
+    pltpu.VMEM((3, 4, 4, 48, 128), BF16),
+    pltpu.VMEM((3, 3, 4, 48, 128), BF16),
+    pltpu.VMEM((3, 4, 48, 128), BF16),
+    pltpu.VMEM((3, 3, 48, 128), BF16),
+    pltpu.VMEM((6, 12, 128), F32),
+    pltpu.VMEM((6, 12, 128), F32),
+]
+
+
+def scatter_kernel(p_ref, dk_ref, dw_ref, dk_out, *scratch):
+    send_sem, recv_sem = scratch[-2:]
+    me = lax.axis_index("seq")
+    greet(me, AXES)
+    net = Net(me, send_sem, recv_sem)
+    rs = Scatter(net, p_ref, *scratch[: len(RS_SCRATCH)])
+    dk = DKernel(net, dk_ref, *scratch[len(RS_SCRATCH) : -2])
+    dk.start()
+    firsts = [rs.start(part) for part in range(3)]
+    dk.to_x()
+    levels = []
+    for part in range(3):
+        rs.add_core(part, firsts[part])
+        levels.append(rs.send_level(part, 0))
+    dk.to_z()
+    for level in range(2):
+        nexts = []
+        for part in range(3):
+            rs.add_level(part, level, levels[part])
+            nexts.append(rs.send_level(part, level + 1))
+        levels = nexts
+        if level == 0:
+            dk.to_y()
+        else:
+            dk.gather_x()
+    totals = [rs.add_level(part, 2, levels[part]) for part in range(3)]
+    rs.exchange(totals)
+    dk.gather_core()
+    rs.finish(dw_ref)
+    dk.finish(dk_out)
+    net.drain()
+
+
+def scatter_all(partial, dk):
+    return pl.pallas_call(
+        scatter_kernel,
+        out_shape=(jax.ShapeDtypeStruct((D // 128, D), F32), jax.ShapeDtypeStruct((K, D), F32)),
+        in_specs=[pl.BlockSpec(memory_space=pltpu.VMEM)] * 2,
+        out_specs=[pl.BlockSpec(memory_space=pltpu.VMEM)] * 2,
+        scratch_shapes=RS_SCRATCH
+        + DK_SCRATCH
+        + [
+            pltpu.SemaphoreType.DMA((48,)),
+            pltpu.SemaphoreType.DMA((48,)),
+        ],
+        compiler_params=pltpu.CompilerParams(
+            collective_id=2, has_side_effects=True, vmem_limit_bytes=60 * 1024 * 1024
+        ),
+    )(partial, dk)
 
 
 def with_halo(block, sides, width):
@@ -45,9 +406,13 @@
         conv_out = conv_out + kernel[tap_index] * padded[
             :, tap_index + 1 : tap_index + 1 + FRAMES_DEV
         ].astype(jnp.float32)
-    bn_mean = lax.psum(jnp.sum(conv_out, axis=(0, 1)), "seq") / frame_total
+    here_mean = jnp.mean(conv_out, axis=(0, 1))
+    here_gap = conv_out - here_mean
+    here_spread = jnp.sum(here_gap * here_gap, axis=(0, 1))
+    stats = reduce_small(jnp.stack([here_mean, here_spread]), True, 0)
+    bn_mean = stats[0]
     deviate = conv_out - bn_mean
-    bn_var = lax.psum(jnp.sum(deviate * deviate, axis=(0, 1)), "seq") / frame_total
+    bn_var = stats[1] / frame_total
     bn_rstd = lax.rsqrt(bn_var + EPSILON)
     normed_bn = deviate * bn_rstd
     bn_out = normed_bn * bn_gain + bn_bias
@@ -60,20 +425,18 @@
         (x_float.reshape(rows_here, D) + branch).astype(jnp.bfloat16).reshape(UTT, FRAMES_DEV, D)
     )
     cot_rows = cotangent.reshape(rows_here, D)
-    d_w_out = lax.psum_scatter(
-        lax.dot_general(
-            cot_rows, act, (((0,), (0,)), ((), ())), preferred_element_type=jnp.float32
-        ),
-        "seq",
-        scatter_dimension=0,
-        tiled=True,
-    )
+    partial = lax.dot_general(
+        cot_rows, act, (((0,), (0,)), ((), ())), preferred_element_type=jnp.float32
+    ).astype(jnp.bfloat16)
+    partial = partial.reshape(64, 24, 2, 3, 2, 128).transpose(2, 3, 0, 4, 1, 5)
+    partial = partial.reshape(2, 3, 4, 4, 4, 48, 128)
     d_act = jnp.dot(cot_rows, w_out, preferred_element_type=jnp.float32)
     d_bn = d_act.reshape(UTT, FRAMES_DEV, D) * (act_sig + bn_out * act_sig * (1.0 - act_sig))
     scaled_grad = d_bn * bn_gain
     local_bias = jnp.sum(d_bn, axis=(0, 1))
     local_gain = jnp.sum(d_bn * normed_bn, axis=(0, 1))
-    d_bn_bias, d_bn_gain = lax.psum((local_bias, local_gain), "seq")
+    sums = reduce_small(jnp.stack([local_bias, local_gain]), False, 1)
+    d_bn_bias, d_bn_gain = sums[0], sums[1]
     mean_grad = bn_gain * d_bn_bias / frame_total
     mean_cross = bn_gain * d_bn_gain / frame_total
     d_conv = bn_rstd * (scaled_grad - mean_grad - normed_bn * mean_cross)
@@ -81,7 +444,8 @@
     for tap_index in range(K):
         window = padded[:, tap_index + 1 : tap_index + 1 + FRAMES_DEV].astype(jnp.float32)
         kernel_rows.append(jnp.sum(window * d_conv, axis=(0, 1)))
-    d_kernel = lax.psum(jnp.stack(kernel_rows), "seq")
+    d_kernel = jnp.stack(kernel_rows)
+    d_kernel = d_kernel.reshape(4, 8, 2, HALF).transpose(2, 0, 1, 3)
     grad_padded = with_halo(d_conv.astype(jnp.bfloat16), (("seq", 1),), 16).astype(d_conv.dtype)
     d_gated = jnp.zeros((UTT, FRAMES_DEV, D), jnp.float32)
     for tap_index in range(K):
@@ -103,6 +467,7 @@
         - ln_hat * jnp.mean(d_hat * ln_hat, axis=-1, keepdims=True)
     )
     d_inputs = (cotangent.astype(jnp.float32) + d_layer).astype(jnp.bfloat16)
+    d_w_out, d_kernel = scatter_all(partial, d_kernel)
     return (outputs, d_inputs, d_w_out, d_kernel, d_bn_gain, d_bn_bias)
 
 

time: 477 us -> 219 us (0.46)
  blocking collectives: 200 us -> 0 us
  waiting for transfers between devices: 132 us -> 3.16 us
  Pallas kernels: 0 us -> 68.8 us
  local copies, waits for them, and re-layouts: 12.7 us -> 31 us
  between operations: 15.4 us -> 2.39 us
    psum x3 -> x0, blocking collectives: 200 us -> none  [the longest x1 73.1 us: on_device(): bn_mean = lax.psum(jnp.sum(conv_out, axis=(0, 1)), 'seq') / frame_total]
    unnamed x2 -> x0, waiting for transfers between devices: 132 us -> none
    pallas_call x0 -> x3, Pallas kernels: none -> 68.8 us  [the longest x1 35.2 us: scatter_all(): pl.pallas_call(scatter_kernel, out_shape=(jax.ShapeDtypeStruct((D // 128,...]
    reshape x0 -> x3, local copies, waits for them, and re-layouts: none -> 11.3 us  [the longest x1 10.5 us: on_device(): partial = partial.reshape(64, 24, 2, 3, 2, 128).transpose(2, 3, 0, 4, 1, 5)]
    convert_element_type x0 -> x1, local copies, waits for them, and re-layouts: none -> 6.71 us  [on_device(): partial = lax.dot_general(cot_rows, act, (((0,), (0,)), ((), ())), prefer...]
    transpose x0 -> x1, local copies, waits for them, and re-layouts: none -> 5.36 us  [on_device(): partial = partial.reshape(64, 24, 2, 3, 2, 128).transpose(2, 3, 0, 4, 1, 5)]
  transfers between devices with their start and end apart: 5 -> 4, of which waited for: 2 -> 1; matrix products, arithmetic and copies ran while one was open for 10% -> 18% of each run, Pallas kernels for 0% -> 16%
where the time goes in v1:
time: 219 us; the launch traced here: 218 us
  Pallas kernels  68.8 us (31%)
  other arithmetic  65.2 us (30%)
  matrix products  34.5 us (16%)
  local copies, waits for them, and re-layouts  31 us (14%)
  starting transfers between devices  13 us (6%)
  waiting for transfers between devices  3.16 us (1%)
  between operations  2.39 us (1%)
    pallas_call x1, Pallas kernels, scatter_all(): pl.pallas_call(scatter_kernel, out_shape=(jax.ShapeDtypeStruct((D // 128,...  35.2 us
    pallas_call x2, Pallas kernels, reduce_small(): pl.pallas_call(functools.partial(reduce_kernel, merge), out_shape=jax.Sha...  33.6 us
    reduce_sum x4, other arithmetic, on_device(): kernel_rows.append(jnp.sum(window * d_conv, axis=(0, 1)))  22 us
    reduce_sum x1, other arithmetic, on_device(): here_mean = jnp.mean(conv_out, axis=(0, 1))  14.8 us
    add x1, other arithmetic, on_device(): d_gated + kernel[tap_index] * grad_padded[:, 31 - tap_index:31 - tap_inde...  12.4 us
    reshape x1, local copies, waits for them, and re-layouts, on_device(): partial = partial.reshape(64, 24, 2, 3, 2, 128).transpose(2, 3, 0, 4, 1, 5)  10.5 us
    dot_general x1, matrix products, on_device(): d_act = jnp.dot(cot_rows, w_out, preferred_element_type=jnp.float32)  9.58 us
    dot_general x1, matrix products, on_device(): lax.dot_general(d_proj, w_in, (((1,), (1,)), ((), ())), preferred_element...  9.16 us
  transfers between devices with their start and end apart: 4, of which 1 were waited for; matrix products, arithmetic and copies ran while one was open for 18% of the time, Pallas kernels for 16%

profile of v1, /device:TPU:1, one launch (start us, length us, event | category | flops | bytes accessed | tf_op | source)
XLA Modules:
  0.0 218.1 jit_solution(5050137864047462446)
XLA Ops:
  0.7 1.8 convert_reduce_fusion
  2.5 2.0 multiply_reduce_fusion.4
  4.5 0.5 multiply_convert_fusion.1
  5.0 0.0 copy-done.77
  5.1 7.6 %fusion.149 = f32[512,3072]{1,0:T(8,128)S(1)} fusion(bf16[512,1536]{1,0:T(8,128)(2,1)S(1)} %bitcast.58, bf16[1536,3072]{1,0:T(8,128)(2,1)} %param.10), kind=kOutput, calls=%fused_computation.339 | convolution fusion | flops 4831838208 | bytes 17301504 | tf_op jit(solution)/shard_map/dot_general | solution.py:399
  12.7 0.8 multiply_convert_fusion
  13.5 1.8 copy-done
  15.3 4.9 %collective-permute-start = (bf16[2,16,1536]{2,1,0:T(8,128)(2,1)S(1)}, bf16[2,16,1536]{2,1,0:T(8,128)(2,1)S(1)}, u32[]{:S(2)}, u32[]{:S(2)}) collective-permute-start(bf16[2,16,1536]{2,1,0:T(8,128)(2,1)S(1)} %get-tuple-element.89), channel_id=1, source_target_pairs={{0,1},{1,2},{2,3},{3,4},{4,5},{5,6},{6,7},{7,8},{8,9},{9,10},{10,1... | collective-permute-start | bytes 294920 | tf_op jit(solution)/shard_map/ppermute | solution.py:381
  20.2 1.9 collective-permute-start.1
  22.2 0.3 slice_reduce_fusion.34
  22.7 0.2 slice_reduce_fusion.33
  23.0 3.1 %collective-permute-done.1 = bf16[2,16,1536]{2,1,0:T(8,128)(2,1)S(1)} collective-permute-done((bf16[2,16,1536]{2,1,0:T(8,128)(2,1)S(1)}, bf16[2,16,1536]{2,1,0:T(8,128)(2,1)S(1)}, u32[]{:S(2)}, u32[]{:S(2)}) %collective-permute-start.1) | collective-permute-done | bytes 98336 | tf_op jit(solution)/shard_map/ppermute | solution.py:384
  26.2 14.8 %fusion.145 = (f32[1536]{0:T(1024)S(1)}, f32[2,256,1536]{2,1,0:T(8,128)S(1)}) fusion(bf16[2,16,1536]{2,1,0:T(8,128)(2,1)S(1)} %collective-permute-done.1, bf16[2,256,1536]{2,1,0:T(8,128)(2,1)S(1)} %bitcast.47, f32[1536]{0:T(1024)S(1)} %get-tuple-element.74, f32[1536]{0:T(1024)S(1)} %get-tuple-element.75, f32[1536]{0:T(1024)S(1)} %get-tuple-element.45, ...), kind=kLoop, calls=%fused_computation.336 | loop fusion | flops 148634112 | bytes 5117952 | tf_op jit(solution)/shard_map/reduce_sum | solution.py:409
  41.0 1.7 copy-done.2
  42.7 0.4 multiply_reduce_fusion.3
  43.4 0.6 pad_maximum_fusion.2.x_ref
  44.0 17.8 %shard_map.127 = f32[2,1536]{1,0:T(2,128)} custom-call(f32[2,1536]{1,0:T(2,128)} %pad_maximum_fusion.2.x_ref), custom_call_target="tpu_custom_call" | custom-call | tf_op jit(solution)/shard_map/pallas_call | solution.py:116
  61.8 0.8 slice_reduce_fusion.2
  62.6 9.6 %fusion.144 = (f32[1536]{0:T(1024)S(1)}, f32[1536]{0:T(1024)S(1)}, bf16[2,256,1536]{2,1,0:T(8,128)(2,1)}, f32[2,256,1536]{2,1,0:T(8,128)}) fusion(f32[1536]{0:T(1024)S(1)} %get-tuple-element.79, f32[2,256,1536]{2,1,0:T(8,128)} %copy-done.2, f32[1536]{0:T(1024)S(1)} %get-tuple-element.78, f32[1536]{0:T(1024)} %param.13, f32[1536]{0:T(1024)} %param.12, ...), kind=kOutput, calls=%fused_computation.335 | convolution fusion | flops 2428498944 | bytes 14192640 | tf_op jit(solution)/shard_map/dot_general | solution.py:433
  72.2 0.6 pad_maximum_fusion.3.x_ref
  72.8 15.8 %shard_map.128 = f32[2,1536]{1,0:T(2,128)} custom-call(f32[2,1536]{1,0:T(2,128)} %pad_maximum_fusion.3.x_ref), custom_call_target="tpu_custom_call" | custom-call | tf_op jit(solution)/shard_map/pallas_call | solution.py:116
  88.7 0.8 slice_reduce_fusion.1
  89.6 0.0 slice-start.2
  89.6 8.1 %fusion.68 = (f32[1536]{0:T(1024)S(1)}, f32[1536]{0:T(1024)S(1)}, f32[1536]{0:T(1024)S(1)}, f32[1536]{0:T(1024)S(1)}, f32[1536]{0:T(1024)S(1)}, /*index=5*/f32[1...) fusion(bf16[2,16,1536]{2,1,0:T(8,128)(2,1)S(1)} %collective-permute-done.1, ...), kind=kLoop, calls=%fused_computation.161 | loop fusion | flops 47958528 | bytes 11194368 | tf_op jit(solution)/shard_map/reduce_sum | solution.py:446
  97.7 0.0 slice-start.3
  97.8 7.1 %fusion.53 = (f32[1536]{0:T(1024)S(1)}, f32[1536]{0:T(1024)S(1)}, f32[1536]{0:T(1024)S(1)}, f32[1536]{0:T(1024)S(1)}, f32[1536]{0:T(1024)S(1)}, /*index=5*/f32[1...) fusion(f32[2,256,1536]{2,1,0:T(8,128)S(1)} %get-tuple-element.80, ...), kind=kLoop, calls=%fused_computation.146 | loop fusion | flops 40095744 | bytes 12730368 | tf_op jit(solution)/shard_map/reduce_sum | solution.py:446
  104.8 4.1 %collective-permute-start.2 = (bf16[2,16,1536]{2,1,0:T(8,128)(2,1)S(1)}, bf16[2,16,1536]{2,1,0:T(8,128)(2,1)S(1)}, u32[]{:S(2)}, u32[]{:S(2)}) collective-permute-start(bf16[2,16,1536]{2,1,0:T(8,128)(2,1)S(1)} %get-tuple-element.87), channel_id=1, source_target_pairs={{0,1},{1,2},{2,3},{3,4},{4,5},{5,6},{6,7},{7,8},{8,9},{9,10},{10,1... | collective-permute-start | bytes 294920 | tf_op jit(solution)/shard_map/ppermute | solution.py:381
  108.9 2.1 collective-permute-start.3
  111.1 3.8 %fusion.111 = bf16[512,1536]{1,0:T(8,128)(2,1)} fusion(bf16[512,1536]{1,0:T(8,128)(2,1)S(1)} %bitcast.63, bf16[1536,1536]{1,0:T(8,128)(2,1)S(1)} %bitcast.61, bf16[512,1536]{1,0:T(8,128)(2,1)S(1)} %bitcast.54), kind=kOutput, calls=%fused_computation.251 | convolution fusion | flops 2418278400 | bytes 9437184 | tf_op jit(solution)/shard_map/dot_general | solution.py:421
  114.8 2.8 %fusion.36 = (f32[1536]{0:T(1024)S(1)}, f32[1536]{0:T(1024)S(1)}, f32[1536]{0:T(1024)S(1)}, f32[1536]{0:T(1024)S(1)}, f32[1536]{0:T(1024)S(1)}, /*index=5*/f32[1536]{0:T(1024)S(1)}) fusion(f32[2,256,1536]{2,1,0:T(8,128)S(1)} %get-tuple-element.80, bf16[2,256,1536]{2,1,0:T(8,128)(2,1)S(1)} %bitcast.50, bf16[2,16,1536]{2,1,0:T(8,128)(2,1)S(1)} %collective-permute-done), kind=kLoop, calls=%fused_computation.129 | loop fusion | flops 28302336 | bytes 4853760 | tf_op jit(solution)/shard_map/reduce_sum | solution.py:446
  117.6 4.1 %fusion.45 = (f32[1536]{0:T(1024)S(1)}, f32[1536]{0:T(1024)S(1)}, f32[1536]{0:T(1024)S(1)}, f32[1536]{0:T(1024)S(1)}, f32[1536]{0:T(1024)S(1)}, /*index=5*/f32[1...) fusion(f32[2,256,1536]{2,1,0:T(8,128)S(1)} %get-tuple-element.80, ...), kind=kLoop, calls=%fused_computation.138 | loop fusion | flops 42453504 | bytes 4872192 | tf_op jit(solution)/shard_map/reduce_sum | solution.py:446
  121.7 4.5 %fusion = bf16[1536,1536]{0,1:T(8,128)(2,1)} fusion(bf16[2,256,1536]{2,1,0:T(8,128)(2,1)S(1)} %copy-done.80, bf16[2,256,1536]{2,1,0:T(8,128)(2,1)S(1)} %copy-done.6), kind=kOutput, calls=%fused_computation.30 | convolution fusion | flops 2418278400 | bytes 7864320 | tf_op jit(solution)/shard_map/dot_general | solution.py:428
  126.6 0.3 stack.152
  126.9 0.1 reshape.143
  127.1 0.7 copy.22
  127.8 6.7 %copy.17 = bf16[1536,1536]{1,0:T(8,128)(2,1)} copy(bf16[1536,1536]{0,1:T(8,128)(2,1)} %fusion) | data formatting | bytes 9437184 | tf_op jit(solution)/shard_map/convert_element_type | solution.py:430
  134.5 10.5 %reshape.141 = bf16[64,24,2,3,2,128]{5,4,3,2,1,0:T(2,128)(2,1)} reshape(bf16[1536,1536]{1,0:T(8,128)(2,1)} %copy.17) | data formatting | bytes 9437184 | tf_op jit(solution)/shard_map/reshape | solution.py:431
  145.0 5.4 %copy.18 = bf16[2,3,64,2,24,128]{5,4,3,2,1,0:T(8,128)(2,1)} copy(bf16[2,3,64,2,24,128]{5,3,1,0,4,2:T(2,128)(2,1)} %bitcast.56) | data formatting | bytes 9437184 | tf_op jit(solution)/shard_map/transpose | solution.py:431
  150.4 35.2 %shard_map.129 = (f32[12,1536]{1,0:T(8,128)}, f32[32,1536]{1,0:T(8,128)}) custom-call(bf16[2,3,4,4,4,48,128]{6,5,4,3,2,1,0:T(8,128)(2,1)} %bitcast.55, f32[2,4,8,768]{3,2,1,0:T(8,128)} %bitcast.59), custom_call_target="tpu_custom_call" | custom-call | tf_op jit(solution)/shard_map/pallas_call | solution.py:359
  186.0 1.5 maximum_convert_fusion
  187.8 12.4 %fusion.69 = f32[2,256,1536]{2,1,0:T(8,128)S(1)} fusion(f32[2,288,1536]{2,1,0:T(8,128)S(1)} %maximum_convert_fusion, f32[1536]{0:T(1024)S(1)} %copy-done.68, f32[1536]{0:T(1024)S(1)} %copy-done.70, f32[1536]{0:T(1024)S(1)} %get-tuple-element.45, f32[1536]{0:T(1024)S(1)} %copy-done.12, f32[1536]{0:T(1024)S(1)} %copy-done.14, f32[1536]{0:T(1024)S(1)} %copy-done.16, ...), kind=kLoop, calls=%fused_computation.163 | loop fusion | flops 49545216 | bytes 104005632 | tf_op jit(solution)/shard_map/add | solution.py:453
  200.2 1.6 fusion.107
  201.8 9.2 %multiply_reduce_fusion.1 = (f32[512]{0:T(512)S(1)}, f32[512,1536]{1,0:T(8,128)}) fusion(f32[1536]{0:T(1024)S(1)} %copy-done.72, bf16[1536,3072]{1,0:T(8,128)(2,1)} %param.10, bf16[512,1536]{1,0:T(8,128)(2,1)S(1)} %get-tuple-element.84, bf16[512,1536]{1,0:T(8,128)(2,1)S(1)} %get-tuple-element.83), kind=kOutput, calls=%fused_computation.241 | convolution fusion | flops 4839702016 | bytes 15736832 | tf_op jit(solution)/shard_map/dot_general | solution.py:460
  211.0 2.8 %multiply_reduce_fusion = f32[2,256]{1,0:T(2,128)S(1)} fusion(f32[2,256,1536]{2,1,0:T(8,128)} %bitcast.57, bf16[2,256,1536]{2,1,0:T(8,128)(2,1)S(1)} %copy-done.1, f32[1536]{0:T(1024)S(1)} %copy-done.72, f32[2,256]{1,0:T(2,128)S(1)} %copy-done.78, f32[2,256]{1,0:T(2,128)S(1)} %copy-done.74), kind=kLoop, calls=%fused_computation.240 | loop fusion | flops 4718080 | bytes 4730880 | tf_op jit(solution)/shard_map/reduce_sum | solution.py:467
  213.8 0.5 copy-done.3
  214.3 2.4 %add_convert_fusion = bf16[2,256,1536]{2,1,0:T(8,128)(2,1)} fusion(bf16[2,256,1536]{2,1,0:T(8,128)(2,1)S(1)} %copy-done.7, bf16[2,256,1536]{2,1,0:T(8,128)(2,1)S(1)} %copy-done.1, f32[2,256]{1,0:T(2,128)S(1)} %broadcast_multiply_fusion.2, f32[2,256]{1,0:T(2,128)S(1)} %div.48, f32[1536]{0:T(1024)S(1)} %copy-done.72, f32[2,256]{1,0:T(2,128)S(1)} %copy-done.78, ...), kind=kLoop, calls=%fused_computation.239 | loop fusion | flops 8650752 | bytes 7878656 | tf_op jit(solution)/shard_map/convert_element_type | solution.py:469
  216.7 0.6 copy.25
  217.4 0.7 copy.26
  (214 shorter events, 0.7 us)
Async XLA Ops:
  12.6 9.5 %copy-start.9 = (f32[32,1536]{1,0:T(8,128)S(1)}, f32[32,1536]{1,0:T(8,128)}, u32[]{:S(2)}) copy-start(f32[32,1536]{1,0:T(8,128)} %param.11) | copy-start | bytes 589828
  15.3 7.7 %collective-permute-start = (bf16[2,16,1536]{2,1,0:T(8,128)(2,1)S(1)}, bf16[2,16,1536]{2,1,0:T(8,128)(2,1)S(1)}, u32[]{:S(2)}, u32[]{:S(2)}) collective-permute-start(bf16[2,16,1536]{2,1,0:T(8,128)(2,1)S(1)} %get-tuple-element.89), channel_id=1, source_target_pairs={{0,1},{1,2},{2,3},{3,4},{4,5},{5,6},{6,7},{7,8},{8,9},{9,10},{10,1... | collective-permute-start | bytes 294920 | tf_op jit(solution)/shard_map/ppermute | solution.py:381
  20.2 5.9 %collective-permute-start.1 = (bf16[2,16,1536]{2,1,0:T(8,128)(2,1)S(1)}, bf16[2,16,1536]{2,1,0:T(8,128)(2,1)S(1)}, u32[]{:S(2)}, u32[]{:S(2)}) collective-permute-start(bf16[2,16,1536]{2,1,0:T(8,128)(2,1)S(1)} %get-tuple-element.90), channel_id=1, source_target_pairs={{1,0},{2,1},{3,2},{4,3},{5,4},{6,5},{7,6},{8,7},{9,8},{10,9},{11,1... | collective-permute-start | bytes 294920 | tf_op jit(solution)/shard_map/ppermute | solution.py:384
  22.5 20.6 %copy-start.11 = (f32[1536]{0:T(1024)}, f32[1536]{0:T(1024)S(1)}, u32[]{:S(2)}) copy-start(f32[1536]{0:T(1024)S(1)} %get-tuple-element.46) | copy-start | bytes 18436
  22.5 20.6 %copy-start.13 = (f32[1536]{0:T(1024)}, f32[1536]{0:T(1024)S(1)}, u32[]{:S(2)}) copy-start(f32[1536]{0:T(1024)S(1)} %get-tuple-element.47) | copy-start | bytes 18436
  22.5 20.6 %copy-start.15 = (f32[1536]{0:T(1024)}, f32[1536]{0:T(1024)S(1)}, u32[]{:S(2)}) copy-start(f32[1536]{0:T(1024)S(1)} %get-tuple-element.48) | copy-start | bytes 18436
  22.5 20.6 %copy-start.17 = (f32[1536]{0:T(1024)}, f32[1536]{0:T(1024)S(1)}, u32[]{:S(2)}) copy-start(f32[1536]{0:T(1024)S(1)} %get-tuple-element.49) | copy-start | bytes 18436
  22.5 20.6 %copy-start.19 = (f32[1536]{0:T(1024)}, f32[1536]{0:T(1024)S(1)}, u32[]{:S(2)}) copy-start(f32[1536]{0:T(1024)S(1)} %get-tuple-element.50) | copy-start | bytes 18436
  22.5 20.6 %copy-start.21 = (f32[1536]{0:T(1024)}, f32[1536]{0:T(1024)S(1)}, u32[]{:S(2)}) copy-start(f32[1536]{0:T(1024)S(1)} %get-tuple-element.51) | copy-start | bytes 18436
  22.6 20.6 %copy-start.23 = (f32[1536]{0:T(1024)}, f32[1536]{0:T(1024)S(1)}, u32[]{:S(2)}) copy-start(f32[1536]{0:T(1024)S(1)} %get-tuple-element.52) | copy-start | bytes 18436
  22.6 20.6 %copy-start.25 = (f32[1536]{0:T(1024)}, f32[1536]{0:T(1024)S(1)}, u32[]{:S(2)}) copy-start(f32[1536]{0:T(1024)S(1)} %get-tuple-element.53) | copy-start | bytes 18436
  22.6 20.6 %copy-start.27 = (f32[1536]{0:T(1024)}, f32[1536]{0:T(1024)S(1)}, u32[]{:S(2)}) copy-start(f32[1536]{0:T(1024)S(1)} %get-tuple-element.54) | copy-start | bytes 18436
  22.6 20.6 %copy-start.29 = (f32[1536]{0:T(1024)}, f32[1536]{0:T(1024)S(1)}, u32[]{:S(2)}) copy-start(f32[1536]{0:T(1024)S(1)} %get-tuple-element.55) | copy-start | bytes 18436
  22.6 20.6 %copy-start.31 = (f32[1536]{0:T(1024)}, f32[1536]{0:T(1024)S(1)}, u32[]{:S(2)}) copy-start(f32[1536]{0:T(1024)S(1)} %get-tuple-element.56) | copy-start | bytes 18436
  22.6 20.6 %copy-start.33 = (f32[1536]{0:T(1024)}, f32[1536]{0:T(1024)S(1)}, u32[]{:S(2)}) copy-start(f32[1536]{0:T(1024)S(1)} %get-tuple-element.57) | copy-start | bytes 18436
  22.6 20.6 %copy-start.35 = (f32[1536]{0:T(1024)}, f32[1536]{0:T(1024)S(1)}, u32[]{:S(2)}) copy-start(f32[1536]{0:T(1024)S(1)} %get-tuple-element.58) | copy-start | bytes 18436
  22.6 20.6 %copy-start.37 = (f32[1536]{0:T(1024)}, f32[1536]{0:T(1024)S(1)}, u32[]{:S(2)}) copy-start(f32[1536]{0:T(1024)S(1)} %get-tuple-element.59) | copy-start | bytes 18436
  22.6 20.6 %copy-start.39 = (f32[1536]{0:T(1024)}, f32[1536]{0:T(1024)S(1)}, u32[]{:S(2)}) copy-start(f32[1536]{0:T(1024)S(1)} %get-tuple-element.60) | copy-start | bytes 18436
  22.6 20.6 %copy-start.41 = (f32[1536]{0:T(1024)}, f32[1536]{0:T(1024)S(1)}, u32[]{:S(2)}) copy-start(f32[1536]{0:T(1024)S(1)} %get-tuple-element.61) | copy-start | bytes 18436
  22.7 20.6 %copy-start.43 = (f32[1536]{0:T(1024)}, f32[1536]{0:T(1024)S(1)}, u32[]{:S(2)}) copy-start(f32[1536]{0:T(1024)S(1)} %get-tuple-element.62) | copy-start | bytes 18436
  22.9 20.4 %copy-start.45 = (f32[1536]{0:T(1024)}, f32[1536]{0:T(1024)S(1)}, u32[]{:S(2)}) copy-start(f32[1536]{0:T(1024)S(1)} %get-tuple-element.63) | copy-start | bytes 18436
  22.9 20.4 %copy-start.47 = (f32[1536]{0:T(1024)}, f32[1536]{0:T(1024)S(1)}, u32[]{:S(2)}) copy-start(f32[1536]{0:T(1024)S(1)} %get-tuple-element.64) | copy-start | bytes 18436
  22.9 20.4 %copy-start.49 = (f32[1536]{0:T(1024)}, f32[1536]{0:T(1024)S(1)}, u32[]{:S(2)}) copy-start(f32[1536]{0:T(1024)S(1)} %get-tuple-element.65) | copy-start | bytes 18436
  22.9 20.4 %copy-start.51 = (f32[1536]{0:T(1024)}, f32[1536]{0:T(1024)S(1)}, u32[]{:S(2)}) copy-start(f32[1536]{0:T(1024)S(1)} %get-tuple-element.66) | copy-start | bytes 18436
  22.9 20.4 %copy-start.53 = (f32[1536]{0:T(1024)}, f32[1536]{0:T(1024)S(1)}, u32[]{:S(2)}) copy-start(f32[1536]{0:T(1024)S(1)} %get-tuple-element.67) | copy-start | bytes 18436
  22.9 20.4 %copy-start.55 = (f32[1536]{0:T(1024)}, f32[1536]{0:T(1024)S(1)}, u32[]{:S(2)}) copy-start(f32[1536]{0:T(1024)S(1)} %get-tuple-element.68) | copy-start | bytes 18436
  22.9 20.4 %copy-start.57 = (f32[1536]{0:T(1024)}, f32[1536]{0:T(1024)S(1)}, u32[]{:S(2)}) copy-start(f32[1536]{0:T(1024)S(1)} %get-tuple-element.69) | copy-start | bytes 18436
  23.0 20.4 %copy-start.59 = (f32[1536]{0:T(1024)}, f32[1536]{0:T(1024)S(1)}, u32[]{:S(2)}) copy-start(f32[1536]{0:T(1024)S(1)} %get-tuple-element.70) | copy-start | bytes 18436
  23.0 20.4 %copy-start.61 = (f32[1536]{0:T(1024)}, f32[1536]{0:T(1024)S(1)}, u32[]{:S(2)}) copy-start(f32[1536]{0:T(1024)S(1)} %get-tuple-element.71) | copy-start | bytes 18436
  23.0 20.4 %copy-start.63 = (f32[1536]{0:T(1024)}, f32[1536]{0:T(1024)S(1)}, u32[]{:S(2)}) copy-start(f32[1536]{0:T(1024)S(1)} %get-tuple-element.72) | copy-start | bytes 18436
  23.0 20.4 %copy-start.65 = (f32[1536]{0:T(1024)}, f32[1536]{0:T(1024)S(1)}, u32[]{:S(2)}) copy-start(f32[1536]{0:T(1024)S(1)} %get-tuple-element.73) | copy-start | bytes 18436
  23.0 20.4 %copy-start.67 = (f32[1536]{0:T(1024)}, f32[1536]{0:T(1024)S(1)}, u32[]{:S(2)}) copy-start(f32[1536]{0:T(1024)S(1)} %get-tuple-element.74) | copy-start | bytes 18436
  23.0 20.4 %copy-start.69 = (f32[1536]{0:T(1024)}, f32[1536]{0:T(1024)S(1)}, u32[]{:S(2)}) copy-start(f32[1536]{0:T(1024)S(1)} %get-tuple-element.75) | copy-start | bytes 18436
  62.6 26.9 %copy-start.79 = (f32[1536]{0:T(1024)S(1)}, f32[1536]{0:T(1024)}, u32[]{:S(2)}) copy-start(f32[1536]{0:T(1024)} %param.12) | copy-start | bytes 18436
  89.5 8.2 %copy-start.75 = (f32[1536]{0:T(1024)}, f32[1536]{0:T(1024)S(1)}, u32[]{:S(2)}) copy-start(f32[1536]{0:T(1024)S(1)} %get-tuple-element.107) | copy-start | bytes 18436
  89.5 8.2 %copy-start.76 = (f32[1536]{0:T(1024)}, f32[1536]{0:T(1024)S(1)}, u32[]{:S(2)}) copy-start(f32[1536]{0:T(1024)S(1)} %get-tuple-element.106) | copy-start | bytes 18436
  89.6 21.5 %slice-start.2 = ((s8[4718592]{0:T(1024)(128)(4,1)}), s8[4194304]{0:T(1024)(128)(4,1)S(1)}, s32[]{:S(2)}) async-start(s8[4718592]{0:T(1024)(128)(4,1)} %bitcast.60), calls=%async_computation.2 | async-start | bytes 8388608
  97.7 13.3 %slice-start.3 = ((s8[4718592]{0:T(1024)(128)(4,1)}), s8[524288]{0:T(1024)(128)(4,1)S(1)}, s32[]{:S(2)}) async-start(s8[4718592]{0:T(1024)(128)(4,1)} %bitcast.60), calls=%async_computation.3 | async-start | bytes 1048576
  97.7 13.3 %copy-start.80 = (bf16[2,256,1536]{2,1,0:T(8,128)(2,1)S(1)}, bf16[2,256,1536]{2,1,0:T(8,128)(2,1)}, u32[]{:S(2)}) copy-start(bf16[2,256,1536]{2,1,0:T(8,128)(2,1)} %get-tuple-element.85) | copy-start | bytes 4718596
  104.8 10.0 %copy-start.4 = (bf16[2,256,1536]{2,1,0:T(8,128)(2,1)}, bf16[2,256,1536]{2,1,0:T(8,128)(2,1)S(1)}, u32[]{:S(2)}) copy-start(bf16[2,256,1536]{2,1,0:T(8,128)(2,1)S(1)} %get-tuple-element.86) | copy-start | bytes 4718596
  104.8 81.1 %collective-permute-start.2 = (bf16[2,16,1536]{2,1,0:T(8,128)(2,1)S(1)}, bf16[2,16,1536]{2,1,0:T(8,128)(2,1)S(1)}, u32[]{:S(2)}, u32[]{:S(2)}) collective-permute-start(bf16[2,16,1536]{2,1,0:T(8,128)(2,1)S(1)} %get-tuple-element.87), channel_id=1, source_target_pairs={{0,1},{1,2},{2,3},{3,4},{4,5},{5,6},{6,7},{7,8},{8,9},{9,10},{10,1... | collective-permute-start | bytes 294920 | tf_op jit(solution)/shard_map/ppermute | solution.py:381
  108.9 77.0 %collective-permute-start.3 = (bf16[2,16,1536]{2,1,0:T(8,128)(2,1)S(1)}, bf16[2,16,1536]{2,1,0:T(8,128)(2,1)}, u32[]{:S(2)}, u32[]{:S(2)}) collective-permute-start(bf16[2,16,1536]{2,1,0:T(8,128)(2,1)S(1)} %get-tuple-element.88), channel_id=1, source_target_pairs={{1,0},{2,1},{3,2},{4,3},{5,4},{6,5},{7,6},{8,7},{9,8},{10,9},{11,1... | collective-permute-start | bytes 294920 | tf_op jit(solution)/shard_map/ppermute | solution.py:384
  117.6 4.1 %copy-start.6 = (bf16[2,256,1536]{2,1,0:T(8,128)(2,1)S(1)}, bf16[2,256,1536]{2,1,0:T(8,128)(2,1)}, u32[]{:S(2)}) copy-start(bf16[2,256,1536]{2,1,0:T(8,128)(2,1)} %param.15) | copy-start | bytes 4718596
  150.4 35.6 %copy-start.5 = (bf16[2,256,1536]{2,1,0:T(8,128)(2,1)S(1)}, bf16[2,256,1536]{2,1,0:T(8,128)(2,1)}, u32[]{:S(2)}) copy-start(bf16[2,256,1536]{2,1,0:T(8,128)(2,1)} %copy-done.4) | copy-start | bytes 4718596
  185.9 14.2 %slice-start = ((s8[6291456]{0:T(1024)(128)(4,1)}), s8[4194304]{0:T(1024)(128)(4,1)S(1)}, s32[]{:S(2)}) async-start(s8[6291456]{0:T(1024)(128)(4,1)} %bitcast.52), calls=%async_computation | async-start | bytes 8388608
  187.8 12.4 %slice-start.1 = ((s8[6291456]{0:T(1024)(128)(4,1)}), s8[2097152]{0:T(1024)(128)(4,1)S(1)}, s32[]{:S(2)}) async-start(s8[6291456]{0:T(1024)(128)(4,1)} %bitcast.52), calls=%async_computation.1 | async-start | bytes 4194304
  201.8 9.2 %copy-start.74 = (f32[2,256]{1,0:T(2,128)S(1)}, f32[2,256]{1,0:T(2,128)}, u32[]{:S(2)}) copy-start(f32[2,256]{1,0:T(2,128)} %copy-done.73) | copy-start | bytes 6148
  201.8 9.2 %copy-start.78 = (f32[2,256]{1,0:T(2,128)S(1)}, f32[2,256]{1,0:T(2,128)}, u32[]{:S(2)}) copy-start(f32[2,256]{1,0:T(2,128)} %copy-done.77) | copy-start | bytes 6148
  (41 other events, 84.1 us)

commit v2 on v1

--- a/solution.py
+++ b/solution.py
@@ -84,48 +84,6 @@
         gap = p[0:1] - mean
         spread = spread + rows * gap * gap
     return jnp.concatenate([mean, spread], axis=0)
-
-
-def reduce_kernel(merge, x_ref, o_ref, cur, got, send_sem, recv_sem):
-    me = lax.axis_index("seq")
-    greet(me, AXES)
-    net = Net(me, send_sem, recv_sem)
-    value = x_ref[...]
-    rows = UTT * FRAMES_DEV
-    slot = 0
-    for level, axis in enumerate(AXES):
-        cur[level] = value
-        copies = []
-        for _, device in peers(me, axis):
-            copies.append((net.send(cur.at[level], got.at[slot], device), slot))
-            slot += 1
-        parts = [value]
-        for copy, index in copies:
-            copy.wait_recv()
-            parts.append(got[index])
-        if merge:
-            value = merge_stats(parts, float(rows))
-        else:
-            value = functools.reduce(jnp.add, parts)
-        rows *= SIZE[axis]
-    o_ref[...] = value
-    net.drain()
-
-
-def reduce_small(x, merge, collective_id):
-    return pl.pallas_call(
-        functools.partial(reduce_kernel, merge),
-        out_shape=jax.ShapeDtypeStruct((2, D), F32),
-        in_specs=[pl.BlockSpec(memory_space=pltpu.VMEM)],
-        out_specs=pl.BlockSpec(memory_space=pltpu.VMEM),
-        scratch_shapes=[
-            pltpu.VMEM((4, 2, D), F32),
-            pltpu.VMEM((10, 2, D), F32),
-            pltpu.SemaphoreType.DMA((10,)),
-            pltpu.SemaphoreType.DMA((10,)),
-        ],
-        compiler_params=pltpu.CompilerParams(collective_id=collective_id, has_side_effects=True),
-    )(x)
 
 
 class DKernel:
@@ -322,153 +280,545 @@
 ]
 
 
-def scatter_kernel(p_ref, dk_ref, dw_ref, dk_out, *scratch):
-    send_sem, recv_sem = scratch[-2:]
+class Reduce:
+    def __init__(self, net, merge, cur, got):
+        self.net, self.merge, self.cur, self.got = net, merge, cur, got
+        self.rows, self.level, self.slot = float(UTT * FRAMES_DEV), 0, 0
+
+    def start(self, value):
+        self.value = value
+        self.cur[self.level] = value
+        self.copies = []
+        for _, device in peers(self.net.me, AXES[self.level]):
+            self.copies.append(
+                (self.net.send(self.cur.at[self.level], self.got.at[self.slot], device), self.slot)
+            )
+            self.slot += 1
+
+    def take(self):
+        parts = [self.value]
+        for copy, index in self.copies:
+            copy.wait_recv()
+            parts.append(self.got[index])
+        if self.merge:
+            value = merge_stats(parts, self.rows)
+        else:
+            value = functools.reduce(jnp.add, parts)
+        self.rows *= SIZE[AXES[self.level]]
+        self.level += 1
+        return value
+
+    def step(self):
+        self.start(self.take())
+
+
+ROWS = UTT * FRAMES_DEV
+CHUNK = 256
+CHUNKS = D // CHUNK
+HALO = 16
+OWN = HALO * 8
+
+
+def dot(a, b):
+    return jnp.dot(a, b, preferred_element_type=F32)
+
+
+def dot_t(a, b):
+    return lax.dot_general(a, b, (((1,), (1,)), ((), ())), preferred_element_type=F32)
+
+
+def span(index, size):
+    return pl.ds(pl.multiple_of(index * size, size), size)
+
+
+def frame_of(row):
+    return (row & 7) * 32 + (row >> 3)
+
+
+def fold(x):
+    return jnp.sum(x.reshape(x.shape[0] // 8, 8, x.shape[1]), axis=0)
+
+
+class Halo:
+    def __init__(self, me, devices, out, got, send_sem, recv_sem):
+        self.out, self.got, self.send_sem, self.recv_sem = out, got, send_sem, recv_sem
+        self.right = lax.rem(me + 1, devices)
+        self.left = lax.rem(me + devices - 1, devices)
+
+    def copies(self, c):
+        return [
+            pltpu.make_async_remote_copy(
+                src_ref=self.out.at[c, way],
+                dst_ref=self.got.at[c, way],
+                send_sem=self.send_sem.at[c, way],
+                recv_sem=self.recv_sem.at[c, way],
+                device_id=(device,),
+                device_id_type=pl.DeviceIdType.MESH,
+            )
+            for way, device in enumerate((self.right, self.left))
+        ]
+
+    def push(self, c, select, blocks):
+        for u in range(UTT):
+            edge = dot(select[...], blocks[u]).astype(BF16)
+            self.out[c, 0, u] = edge[0:HALO]
+            self.out[c, 1, u] = edge[HALO : 2 * HALO]
+        for copy in self.copies(c):
+            copy.start()
+
+    def wait(self, c):
+        for copy in self.copies(c):
+            copy.wait_recv()
+
+    def drain(self):
+        for c in range(CHUNKS):
+            for copy in self.copies(c):
+                copy.wait_send()
+
+
+def extend(ext, u, cols, low, high, row_id):
+    for j in range(HALO):
+        below = pltpu.roll(ext[u, OWN + (16 + j) * 8 : OWN + (17 + j) * 8, cols], 1, 0)
+        ext[u, j * 8 : j * 8 + 8, cols] = jnp.where(row_id == 0, low[j : j + 1], below)
+        above = pltpu.roll(ext[u, OWN + j * 8 : OWN + j * 8 + 8, cols], 7, 0)
+        ext[u, (48 + j) * 8 : (49 + j) * 8, cols] = jnp.where(row_id == 7, high[j : j + 1], above)
+
+
+def convolve(ext, u, cols, taps, forward):
+    for base in range(0, 32, 8):
+        acc = [None] * 8
+        reach = range(base + 1, base + 40) if forward else range(base, base + 39)
+        for e in reach:
+            x = ext[u, e * 8 : e * 8 + 8, cols]
+            for o in range(8):
+                k = e - (base + o) - 1 if forward else base + o + 31 - e
+                if 0 <= k < K:
+                    term = taps[k] * x
+                    acc[o] = term if acc[o] is None else acc[o] + term
+        yield base, acc
+
+
+def whole_kernel(n_dev, x_hbm, lng_ref, win_hbm, ker_ref, bng_ref, bnb_ref, wout_hbm, cot_hbm,
+                 out_hbm, din_hbm, dw_ref, dk_ref, dbn_ref, *scratch):
+    s = dict(zip([name for name, _ in SCRATCH], scratch))
     me = lax.axis_index("seq")
-    greet(me, AXES)
-    net = Net(me, send_sem, recv_sem)
-    rs = Scatter(net, p_ref, *scratch[: len(RS_SCRATCH)])
-    dk = DKernel(net, dk_ref, *scratch[len(RS_SCRATCH) : -2])
+    local = s["local_sem"]
+    loads = [
+        pltpu.make_async_copy(x_hbm, s["x_raw"], local.at[0]),
+        pltpu.make_async_copy(win_hbm, s["w_in"], local.at[1]),
+        pltpu.make_async_copy(cot_hbm, s["cot_raw"], local.at[2]),
+        pltpu.make_async_copy(wout_hbm, s["w_out"], local.at[3]),
+    ]
+    for load in loads:
+        load.start()
+    net = Net(me, s["send_sem"], s["recv_sem"])
+    halo1 = Halo(me, n_dev, s["h_out1"], s["h_got1"], s["h_send1"], s["h_recv1"])
+    halo2 = Halo(me, n_dev, s["h_out2"], s["h_got2"], s["h_send2"], s["h_recv2"])
+
+    perm, perm_t, eye, select = s["perm"], s["perm_t"], s["eye"], s["select"]
+    r0 = lax.broadcasted_iota(jnp.int32, (256, 256), 0)
+    r1 = lax.broadcasted_iota(jnp.int32, (256, 256), 1)
+    perm[...] = jnp.where(frame_of(r0) == r1, 1.0, 0.0).astype(BF16)
+    perm_t[...] = jnp.where(frame_of(r1) == r0, 1.0, 0.0).astype(BF16)
+    eye[...] = jnp.where(r0 == r1, 1.0, 0.0).astype(BF16)
+    q0 = lax.broadcasted_iota(jnp.int32, (32, 256), 0)
+    q1 = lax.broadcasted_iota(jnp.int32, (32, 256), 1)
+    edge_frame = jnp.where(q0 < HALO, FRAMES_DEV - HALO + q0, q0 - HALO)
+    select[...] = jnp.where(frame_of(q1) == edge_frame, 1.0, 0.0).astype(BF16)
+    row_id = lax.broadcasted_iota(jnp.int32, (8, 128), 0)
+
+    x_p, normed, mu_ref, rstd_ref = s["x_p"], s["bf"], s["mu"], s["rstd"]
+    loads[0].wait()
+
+    def norm_tile(i, carry):
+        u, part = i // 4, lax.rem(i, 4)
+        rows = span(i, 64)
+        x = dot(perm[span(part, 64), :], s["x_raw"][u])
+        x_p[rows, :] = x.astype(BF16)
+        mean = jnp.mean(x, axis=-1, keepdims=True)
+        gap = x - mean
+        rstd = lax.rsqrt(jnp.mean(gap * gap, axis=-1, keepdims=True) + EPSILON)
+        mu_ref[rows, :] = mean
+        rstd_ref[rows, :] = rstd
+        normed[rows, :] = (gap * rstd * lng_ref[...]).astype(BF16)
+        return carry
+
+    lax.fori_loop(0, 8, norm_tile, 0)
+    greet(me, AXES, (halo1.left, halo1.right))
+    loads[1].wait()
+    w_in, val, gs, ext_g, ext_d = s["w_in"], s["val"], s["gs"], s["ext_g"], s["ext_d"]
+
+    def project(c, carry):
+        cols = span(c, CHUNK)
+        val[:, cols] = dot(normed[...], w_in[:, cols])
+        gate_cols = pl.ds(pl.multiple_of(D + c * CHUNK, CHUNK), CHUNK)
+        gs[:, cols] = dot(normed[...], w_in[:, gate_cols])
+        blocks = []
+        for u in range(UTT):
+            rows = pl.ds(u * 256, 256)
+            sig = jax.nn.sigmoid(gs[rows, cols])
+            gs[rows, cols] = sig
+            gated = (val[rows, cols] * sig).astype(BF16)
+            ext_g[u, OWN : OWN + 256, cols] = gated.astype(F32)
+            blocks.append(gated)
+        halo1.push(c, select, blocks)
+        return carry
+
+    lax.fori_loop(0, CHUNKS, project, 0)
+
+    def halo_rows(halo, c, u, lane):
+        low = halo.got[c, 0, u, :, lane : lane + 128].astype(F32)
+        high = halo.got[c, 1, u, :, lane : lane + 128].astype(F32)
+        return jnp.where(me == 0, 0.0, low), jnp.where(me == n_dev - 1, 0.0, high)
+
+    conv, stat = s["conv"], s["stat"]
+
+    def taps_of(cols):
+        return [jnp.broadcast_to(ker_ref[k : k + 1, cols], (8, 128)) for k in range(K)]
+
+    def conv_chunk(c, carry):
+        halo1.wait(c)
+        for half in range(2):
+            cols = pl.ds(pl.multiple_of(c * CHUNK + half * 128, 128), 128)
+            taps = taps_of(cols)
+            total = jnp.zeros((8, 128), F32)
+            for u in range(UTT):
+                low, high = halo_rows(halo1, c, u, half * 128)
+                extend(ext_g, u, cols, low, high, row_id)
+                for base, acc in convolve(ext_g, u, cols, taps, True):
+                    for o in range(8):
+                        conv[pl.ds(u * 256 + (base + o) * 8, 8), cols] = acc[o]
+                        total = total + acc[o]
+            mean = jnp.sum(total, axis=0, keepdims=True) * (1.0 / ROWS)
+            gap = conv[:, cols] - mean
+            stat[0:1, cols] = mean
+            stat[1:2, cols] = jnp.sum(fold(gap * gap), axis=0, keepdims=True)
+        return carry
+
+    lax.fori_loop(0, CHUNKS, conv_chunk, 0)
+
+    ar1 = Reduce(net, True, s["cur1"], s["ar1"])
+    ar1.start(stat[...])
+    loads[2].wait()
+    cot_p, cot_t, w_out = s["cot_p"], s["cot_t"], s["w_out"]
+
+    def turn(c, carry):
+        cols = span(c, CHUNK)
+        for u in range(UTT):
+            cot_p[u * 256 : u * 256 + 256, cols] = dot(perm[...], s["cot_raw"][u, :, cols]).astype(BF16)
+        cot_t[cols, :] = dot_t(eye[...], cot_p[:, cols]).astype(BF16)
+        return carry
+
+    lax.fori_loop(0, CHUNKS, turn, 0)
+    ar1.step()
+    loads[3].wait()
+
+    def act_grad(c, carry):
+        cols = span(c, CHUNK)
+        res = dot(cot_p[...], w_out[:, cols])
+        for u in range(UTT):
+            ext_d[u, OWN : OWN + 256, cols] = res[u * 256 : u * 256 + 256]
+        return carry
+
+    lax.fori_loop(0, CHUNKS // 2, act_grad, 0)
+    ar1.step()
+    lax.fori_loop(CHUNKS // 2, CHUNKS, act_grad, 0)
+    ar1.step()
+    stats = ar1.take()
+    total_rows = float(ROWS * n_dev)
+    coef = s["coef"]
+    coef[0:1, :] = stats[0:1]
+    coef[1:2, :] = lax.rsqrt(stats[1:2] * (1.0 / total_rows) + EPSILON)
+    act = s["bf"]
+
+    def bn_block(cb, carry):
+        cols = span(cb, 128)
+        mean, rstd = coef[0:1, cols], coef[1:2, cols]
+        gain, bias = bng_ref[:, cols], bnb_ref[:, cols]
+        sum_bias = jnp.zeros((8, 128), F32)
+        sum_gain = jnp.zeros((8, 128), F32)
+        for u in range(UTT):
+            rows = pl.ds(u * 256, 256)
+            xhat = (conv[rows, cols] - mean) * rstd
+            bn = xhat * gain + bias
+            sig = jax.nn.sigmoid(bn)
+            conv[rows, cols] = xhat
+            act[rows, cols] = (bn * sig).astype(BF16)
+            d_bn = ext_d[u, OWN : OWN + 256, cols] * (sig + bn * sig * (1.0 - sig))
+            ext_d[u, OWN : OWN + 256, cols] = d_bn
+            sum_bias = sum_bias + fold(d_bn)
+            sum_gain = sum_gain + fold(d_bn * xhat)
+        stat[0:1, cols] = jnp.sum(sum_gain, axis=0, keepdims=True)
+        stat[1:2, cols] = jnp.sum(sum_bias, axis=0, keepdims=True)
+        return carry
+
+    lax.fori_loop(0, D // 128, bn_block, 0)
+    ar2 = Reduce(net, False, s["cur2"], s["ar2"])
+    ar2.start(stat[...])
+
+    core = coord(me, "core")
+    part_ref = s["part"]
+    rs = Scatter(net, part_ref, *[s[name] for name in RS_NAMES])
+
+    def weight_part(h, p):
+        cols = pl.ds(pl.multiple_of(h * HALF + p * CHUNK, CHUNK), CHUNK)
+
+        def tile(m, carry):
+            res = dot(cot_t[span(m, 192), :], act[:, cols])
+            for j in range(8):
+                piece = res[j * 24 : j * 24 + 24]
+                piece = jnp.concatenate([piece[:, 0:128], piece[:, 128:256]], axis=0).astype(BF16)
+                part_ref[h, p, m // 2, lax.rem(m, 2) * 2 + j // 4, j % 4] = piece
+            return carry
+
+        lax.fori_loop(0, 8, tile, 0)
+
+    firsts = []
+    for p in range(3):
+        weight_part(1 - core, p)
+        firsts.append(rs.start(p))
+    ar2.step()
+    saves = []
+
+    def branch(u):
+        rows = pl.ds(u * 256, 256)
+
+        def tile(n, carry):
+            cols = span(n, CHUNK)
+            res = dot_t(act[rows, :], w_out[cols, :])
+            res = (x_p[rows, cols].astype(F32) + res).astype(BF16)
+            s["x_raw"][u, :, cols] = dot(perm_t[...], res).astype(BF16)
+            return carry
+
+        lax.fori_loop(0, CHUNKS, tile, 0)
+        copy = pltpu.make_async_copy(s["x_raw"].at[u], out_hbm.at[u], local.at[4 + u])
+        copy.start()
+        saves.append(copy)
+
+    branch(0)
+    ar2.step()
+    branch(1)
+    ar2.step()
+    for p in range(3):
+        weight_part(core, p)
+    sums = ar2.take()
+    dbn_ref[...] = sums
+    gain_row = bng_ref[...]
+    rstd_row = coef[1:2, :]
+    coef[2:3, :] = rstd_row * gain_row
+    coef[3:4, :] = rstd_row * (gain_row * sums[1:2] * (1.0 / total_rows))
+    coef[4:5, :] = rstd_row * (gain_row * sums[0:1] * (1.0 / total_rows))
+
+    def conv_grad(c, carry):
+        cols = span(c, CHUNK)
+        blocks = []
+        for u in range(UTT):
+            d_bn = ext_d[u, OWN : OWN + 256, cols]
+            xhat = conv[u * 256 : u * 256 + 256, cols]
+            d_conv = d_bn * coef[2:3, cols] - coef[3:4, cols] - xhat * coef[4:5, cols]
+            ext_d[u, OWN : OWN + 256, cols] = d_conv
+            blocks.append(d_conv.astype(BF16))
+        halo2.push(c, select, blocks)
+        return carry
+
+    lax.fori_loop(0, CHUNKS, conv_grad, 0)
+
+    levels = []
+    for p in range(3):
+        rs.add_core(p, firsts[p])
+        levels.append(rs.send_level(p, 0))
+
+    dk_src = s["dk_src"]
+
+    def kernel_grad(h):
+        def body(n, carry):
+            cols = pl.ds(pl.multiple_of(h * HALF + n * 128, 128), 128)
+            acc = [jnp.zeros((8, 128), F32)] * K
+            for u in range(UTT):
+                for base in range(0, 32, 8):
+                    grads = [
+                        ext_d[u, OWN + (base + o) * 8 : OWN + (base + o) * 8 + 8, cols] for o in range(8)
+                    ]
+                    for e in range(base + 1, base + 40):
+                        x = ext_g[u, e * 8 : e * 8 + 8, cols]
+                        for o in range(8):
+                            k = e - (base + o) - 1
+                            if 0 <= k < K:
+                                acc[k] = acc[k] + x * grads[o]
+            for k in range(K):
+                dk_src[h, k // 8, k % 8 : k % 8 + 1, span(n, 128)] = jnp.sum(acc[k], axis=0, keepdims=True)
+            return carry
+
+        lax.fori_loop(0, HALF // 128, body, 0)
+
+    dk = DKernel(net, dk_src, *[s[name] for name in DK_NAMES])
+    kernel_grad(1 - core)
     dk.start()
-    firsts = [rs.start(part) for part in range(3)]
+    nexts = []
+    for p in range(3):
+        rs.add_level(p, 0, levels[p])
+        nexts.append(rs.send_level(p, 1))
+    kernel_grad(core)
     dk.to_x()
-    levels = []
-    for part in range(3):
-        rs.add_core(part, firsts[part])
-        levels.append(rs.send_level(part, 0))
+    d_proj = s["d_proj"]
+
+    def input_grad(c, carry):
+        halo2.wait(c)
+        for half in range(2):
+            start = pl.multiple_of(c * CHUNK + half * 128, 128)
+            cols = pl.ds(start, 128)
+            gate_cols = pl.ds(pl.multiple_of(D + start, 128), 128)
+            taps = taps_of(cols)
+            for u in range(UTT):
+                low, high = halo_rows(halo2, c, u, half * 128)
+                extend(ext_d, u, cols, low, high, row_id)
+                for base, acc in convolve(ext_d, u, cols, taps, False):
+                    rows = pl.ds(u * 256 + base * 8, 64)
+                    grad = jnp.concatenate(acc, axis=0)
+                    sig = gs[rows, cols]
+                    by_sig = grad * sig
+                    d_proj[rows, cols] = by_sig.astype(BF16)
+                    d_proj[rows, gate_cols] = (by_sig * val[rows, cols] * (1.0 - sig)).astype(BF16)
+        return carry
+
+    lax.fori_loop(0, CHUNKS // 2, input_grad, 0)
+    levels = nexts
+    nexts = []
+    for p in range(3):
+        rs.add_level(p, 1, levels[p])
+        nexts.append(rs.send_level(p, 2))
     dk.to_z()
-    for level in range(2):
-        nexts = []
-        for part in range(3):
-            rs.add_level(part, level, levels[part])
-            nexts.append(rs.send_level(part, level + 1))
-        levels = nexts
-        if level == 0:
-            dk.to_y()
-        else:
-            dk.gather_x()
-    totals = [rs.add_level(part, 2, levels[part]) for part in range(3)]
-    rs.exchange(totals)
+    lax.fori_loop(CHUNKS // 2, CHUNKS, input_grad, 0)
+    rs.exchange([rs.add_level(p, 2, nexts[p]) for p in range(3)])
+    dk.to_y()
+
+    def frame_grad(u):
+        rows_u = pl.ds(u * 256, 256)
+
+        def tile(n, carry):
+            cols = span(n, CHUNK)
+            conv[rows_u, cols] = dot_t(d_proj[rows_u, :], w_in[cols, :])
+            return carry
+
+        lax.fori_loop(0, CHUNKS, tile, 0)
+
+    def norm_grad(u):
+        def tile(i, carry):
+            rows = pl.ds(pl.multiple_of(u * 256 + i * 32, 32), 32)
+            d_hat = conv[rows, :] * lng_ref[...]
+            rstd = rstd_ref[rows, :]
+            hat = (x_p[rows, :].astype(F32) - mu_ref[rows, :]) * rstd
+            m1 = jnp.mean(d_hat, axis=-1, keepdims=True)
+            m2 = jnp.mean(d_hat * hat, axis=-1, keepdims=True)
+            grad = rstd * (d_hat - m1 - hat * m2)
+            act[rows, :] = (cot_p[rows, :].astype(F32) + grad).astype(BF16)
+            return carry
+
+        lax.fori_loop(0, 8, tile, 0)
+
+        def back(n, carry):
+            cols = span(n, CHUNK)
+            s["cot_raw"][u, :, cols] = dot(perm_t[...], act[u * 256 : u * 256 + 256, cols]).astype(BF16)
+            return carry
+
+        lax.fori_loop(0, CHUNKS, back, 0)
+        copy = pltpu.make_async_copy(s["cot_raw"].at[u], din_hbm.at[u], local.at[6 + u])
+        copy.start()
+        saves.append(copy)
+
+    frame_grad(0)
+    dk.gather_x()
+    norm_grad(0)
     dk.gather_core()
+    frame_grad(1)
     rs.finish(dw_ref)
-    dk.finish(dk_out)
+    dk.finish(dk_ref)
+    norm_grad(1)
+    for copy in saves:
+        copy.wait()
     net.drain()
-
-
-def scatter_all(partial, dk):
-    return pl.pallas_call(
-        scatter_kernel,
-        out_shape=(jax.ShapeDtypeStruct((D // 128, D), F32), jax.ShapeDtypeStruct((K, D), F32)),
-        in_specs=[pl.BlockSpec(memory_space=pltpu.VMEM)] * 2,
-        out_specs=[pl.BlockSpec(memory_space=pltpu.VMEM)] * 2,
-        scratch_shapes=RS_SCRATCH
-        + DK_SCRATCH
-        + [
-            pltpu.SemaphoreType.DMA((48,)),
-            pltpu.SemaphoreType.DMA((48,)),
-        ],
+    halo1.drain()
+    halo2.drain()
+
+
+RS_NAMES = ["got_core", "s1", "got1", "s2", "got2", "s3", "got3", "tail", "got_tail"]
+DK_NAMES = ["dk%d" % i for i in range(len(DK_SCRATCH))]
+VM = pltpu.VMEM
+SCRATCH = [
+    ("x_raw", VM((UTT, 256, D), BF16)),
+    ("w_in", VM((D, 2 * D), BF16)),
+    ("cot_raw", VM((UTT, 256, D), BF16)),
+    ("w_out", VM((D, D), BF16)),
+    ("perm", VM((256, 256), BF16)),
+    ("perm_t", VM((256, 256), BF16)),
+    ("eye", VM((256, 256), BF16)),
+    ("select", VM((32, 256), BF16)),
+    ("x_p", VM((ROWS, D), BF16)),
+    ("bf", VM((ROWS, D), BF16)),
+    ("mu", VM((ROWS, 1), F32)),
+    ("rstd", VM((ROWS, 1), F32)),
+    ("val", VM((ROWS, D), F32)),
+    ("gs", VM((ROWS, D), F32)),
+    ("ext_g", VM((UTT, 512, D), F32)),
+    ("ext_d", VM((UTT, 512, D), F32)),
+    ("conv", VM((ROWS, D), F32)),
+    ("stat", VM((2, D), F32)),
+    ("coef", VM((8, D), F32)),
+    ("cot_p", VM((ROWS, D), BF16)),
+    ("cot_t", VM((D, ROWS), BF16)),
+    ("d_proj", VM((ROWS, 2 * D), BF16)),
+    ("part", VM((2, 3, 4, 4, 4, 48, 128), BF16)),
+    ("h_out1", VM((CHUNKS, 2, UTT, HALO, CHUNK), BF16)),
+    ("h_got1", VM((CHUNKS, 2, UTT, HALO, CHUNK), BF16)),
+    ("h_out2", VM((CHUNKS, 2, UTT, HALO, CHUNK), BF16)),
+    ("h_got2", VM((CHUNKS, 2, UTT, HALO, CHUNK), BF16)),
+    ("cur1", VM((4, 2, D), F32)),
+    ("ar1", VM((10, 2, D), F32)),
+    ("cur2", VM((4, 2, D), F32)),
+    ("ar2", VM((10, 2, D), F32)),
+    ("dk_src", VM((2, 4, 8, HALF), F32)),
+]
+SCRATCH += list(zip(RS_NAMES, RS_SCRATCH)) + list(zip(DK_NAMES, DK_SCRATCH))
+SCRATCH += [
+    ("local_sem", pltpu.SemaphoreType.DMA((8,))),
+    ("send_sem", pltpu.SemaphoreType.DMA((72,))),
+    ("recv_sem", pltpu.SemaphoreType.DMA((72,))),
+    ("h_send1", pltpu.SemaphoreType.DMA((CHUNKS, 2))),
+    ("h_recv1", pltpu.SemaphoreType.DMA((CHUNKS, 2))),
+    ("h_send2", pltpu.SemaphoreType.DMA((CHUNKS, 2))),
+    ("h_recv2", pltpu.SemaphoreType.DMA((CHUNKS, 2))),
+]
+
+
+def on_device(inputs, ln_gain, w_in, kernel, bn_gain, bn_bias, w_out, cotangent):
+    any_spec = pl.BlockSpec(memory_space=pl.ANY)
+    vmem_spec = pl.BlockSpec(memory_space=pltpu.VMEM)
+    outputs, d_inputs, d_w_out, d_kernel, d_bn = pl.pallas_call(
+        functools.partial(whole_kernel, lax.axis_size("seq")),
+        out_shape=(
+            jax.ShapeDtypeStruct((UTT, FRAMES_DEV, D), BF16),
+            jax.ShapeDtypeStruct((UTT, FRAMES_DEV, D), BF16),
+            jax.ShapeDtypeStruct((D // 128, D), F32),
+            jax.ShapeDtypeStruct((K, D), F32),
+            jax.ShapeDtypeStruct((2, D), F32),
+        ),
+        in_specs=[any_spec, vmem_spec, any_spec, vmem_spec, vmem_spec, vmem_spec, any_spec, any_spec],
+        out_specs=[any_spec, any_spec, vmem_spec, vmem_spec, vmem_spec],
+        scratch_shapes=[spec for _, spec in SCRATCH],
         compiler_params=pltpu.CompilerParams(
-            collective_id=2, has_side_effects=True, vmem_limit_bytes=60 * 1024 * 1024
+            collective_id=0, has_side_effects=True, vmem_limit_bytes=67043328
         ),
-    )(partial, dk)
-
-
-def with_halo(block, sides, width):
-    for axis, dim in sides:
-        count = lax.axis_size(axis)
-        forward = [(i, i + 1) for i in range(count - 1)]
-        backward = [(target, source) for source, target in forward]
-        low = lax.ppermute(
-            lax.slice_in_dim(block, block.shape[dim] - width, None, axis=dim), axis, forward
-        )
-        high = lax.ppermute(lax.slice_in_dim(block, 0, width, axis=dim), axis, backward)
-        block = jnp.concatenate([low, block, high], axis=dim)
-    return block
-
-
-def on_device(inputs, ln_gain, w_in, kernel, bn_gain, bn_bias, w_out, cotangent):
-    devices_seq = lax.axis_size("seq")
-    frame_total = UTT * FRAMES_DEV * devices_seq
-    rows_here = UTT * FRAMES_DEV
-    x_float = inputs.astype(jnp.float32)
-    ln_mean = jnp.mean(x_float, axis=-1, keepdims=True)
-    centred = x_float - ln_mean
-    ln_rstd = lax.rsqrt(jnp.mean(centred * centred, axis=-1, keepdims=True) + EPSILON)
-    ln_hat = centred * ln_rstd
-    normed = (ln_hat * ln_gain).astype(jnp.bfloat16).reshape(rows_here, D)
-    proj = jnp.dot(normed, w_in, preferred_element_type=jnp.float32)
-    value_half = proj[:, :D]
-    gate_sig = jax.nn.sigmoid(proj[:, D:])
-    gated = (value_half * gate_sig).astype(jnp.bfloat16).reshape(UTT, FRAMES_DEV, D)
-    padded = with_halo(gated, (("seq", 1),), 16)
-    conv_out = jnp.zeros((UTT, FRAMES_DEV, D), jnp.float32)
-    for tap_index in range(K):
-        conv_out = conv_out + kernel[tap_index] * padded[
-            :, tap_index + 1 : tap_index + 1 + FRAMES_DEV
-        ].astype(jnp.float32)
-    here_mean = jnp.mean(conv_out, axis=(0, 1))
-    here_gap = conv_out - here_mean
-    here_spread = jnp.sum(here_gap * here_gap, axis=(0, 1))
-    stats = reduce_small(jnp.stack([here_mean, here_spread]), True, 0)
-    bn_mean = stats[0]
-    deviate = conv_out - bn_mean
-    bn_var = stats[1] / frame_total
-    bn_rstd = lax.rsqrt(bn_var + EPSILON)
-    normed_bn = deviate * bn_rstd
-    bn_out = normed_bn * bn_gain + bn_bias
-    act_sig = jax.nn.sigmoid(bn_out)
-    act = (bn_out * act_sig).astype(jnp.bfloat16).reshape(rows_here, D)
-    branch = lax.dot_general(
-        act, w_out, (((1,), (1,)), ((), ())), preferred_element_type=jnp.float32
+    )(
+        inputs,
+        ln_gain.reshape(1, D),
+        w_in,
+        kernel,
+        bn_gain.reshape(1, D),
+        bn_bias.reshape(1, D),
+        w_out,
+        cotangent,
     )
-    outputs = (
-        (x_float.reshape(rows_here, D) + branch).astype(jnp.bfloat16).reshape(UTT, FRAMES_DEV, D)
-    )
-    cot_rows = cotangent.reshape(rows_here, D)
-    partial = lax.dot_general(
-        cot_rows, act, (((0,), (0,)), ((), ())), preferred_element_type=jnp.float32
-    ).astype(jnp.bfloat16)
-    partial = partial.reshape(64, 24, 2, 3, 2, 128).transpose(2, 3, 0, 4, 1, 5)
-    partial = partial.reshape(2, 3, 4, 4, 4, 48, 128)
-    d_act = jnp.dot(cot_rows, w_out, preferred_element_type=jnp.float32)
-    d_bn = d_act.reshape(UTT, FRAMES_DEV, D) * (act_sig + bn_out * act_sig * (1.0 - act_sig))
-    scaled_grad = d_bn * bn_gain
-    local_bias = jnp.sum(d_bn, axis=(0, 1))
-    local_gain = jnp.sum(d_bn * normed_bn, axis=(0, 1))
-    sums = reduce_small(jnp.stack([local_bias, local_gain]), False, 1)
-    d_bn_bias, d_bn_gain = sums[0], sums[1]
-    mean_grad = bn_gain * d_bn_bias / frame_total
-    mean_cross = bn_gain * d_bn_gain / frame_total
-    d_conv = bn_rstd * (scaled_grad - mean_grad - normed_bn * mean_cross)
-    kernel_rows = []
-    for tap_index in range(K):
-        window = padded[:, tap_index + 1 : tap_index + 1 + FRAMES_DEV].astype(jnp.float32)
-        kernel_rows.append(jnp.sum(window * d_conv, axis=(0, 1)))
-    d_kernel = jnp.stack(kernel_rows)
-    d_kernel = d_kernel.reshape(4, 8, 2, HALF).transpose(2, 0, 1, 3)
-    grad_padded = with_halo(d_conv.astype(jnp.bfloat16), (("seq", 1),), 16).astype(d_conv.dtype)
-    d_gated = jnp.zeros((UTT, FRAMES_DEV, D), jnp.float32)
-    for tap_index in range(K):
-        d_gated = (
-            d_gated
-            + kernel[tap_index] * grad_padded[:, 31 - tap_index : 31 - tap_index + FRAMES_DEV]
-        )
-    d_gated = d_gated.reshape(rows_here, D)
-    d_value = d_gated * gate_sig
-    d_gate = d_gated * value_half * gate_sig * (1.0 - gate_sig)
-    d_proj = jnp.concatenate([d_value, d_gate], axis=-1).astype(jnp.bfloat16)
-    d_normed = lax.dot_general(
-        d_proj, w_in, (((1,), (1,)), ((), ())), preferred_element_type=jnp.float32
-    )
-    d_hat = d_normed.reshape(UTT, FRAMES_DEV, D) * ln_gain
-    d_layer = ln_rstd * (
-        d_hat
-        - jnp.mean(d_hat, axis=-1, keepdims=True)
-        - ln_hat * jnp.mean(d_hat * ln_hat, axis=-1, keepdims=True)
-    )
-    d_inputs = (cotangent.astype(jnp.float32) + d_layer).astype(jnp.bfloat16)
-    d_w_out, d_kernel = scatter_all(partial, d_kernel)
-    return (outputs, d_inputs, d_w_out, d_kernel, d_bn_gain, d_bn_bias)
+    return (outputs, d_inputs, d_w_out, d_kernel, d_bn[0], d_bn[1])
 
 
 def solution(mesh):

time: 219 us -> 117 us (0.53)
  other arithmetic: 65.2 us -> 0 us
  Pallas kernels: 68.8 us -> 104 us
  matrix products: 34.5 us -> 0 us
  local copies, waits for them, and re-layouts: 31 us -> 10.5 us
  starting transfers between devices: 13 us -> 0 us
  waiting for transfers between devices: 3.16 us -> 0 us
    reduce_sum x9 -> x0, other arithmetic: 43.8 us -> none  [the longest x4 22 us: on_device(): kernel_rows.append(jnp.sum(window * d_conv, axis=(0, 1)))]
    pallas_call x3 -> x1, Pallas kernels: 68.8 us -> 104 us  [on_device(): pl.pallas_call(functools.partial(whole_kernel, lax.axis_size('seq')), out...]
    dot_general x5 -> x0, matrix products: 34.5 us -> none  [the longest x1 9.58 us: on_device(): d_act = jnp.dot(cot_rows, w_out, preferred_element_type=jnp.float32)]
    ppermute x4 -> x0, starting transfers between devices: 13 us -> none  [the longest x2 8.97 us: with_halo(): lax.ppermute(lax.slice_in_dim(block, block.shape[dim] - width, None, axis...]
    add x1 -> x0, other arithmetic: 12.4 us -> none  [on_device(): d_gated + kernel[tap_index] * grad_padded[:, 31 - tap_index:31 - tap_inde...]
    reshape x3, local copies, waits for them, and re-layouts: 11.3 us -> 3.88 us  [the longest x1 1.3 us: on_device(): ln_gain.reshape(1, D)]
    convert_element_type x1 -> x0, local copies, waits for them, and re-layouts: 6.71 us -> none  [on_device(): partial = lax.dot_general(cot_rows, act, (((0,), (0,)), ((), ())), prefer...]
    transpose x1 -> x0, local copies, waits for them, and re-layouts: 5.36 us -> none  [on_device(): partial = partial.reshape(64, 24, 2, 3, 2, 128).transpose(2, 3, 0, 4, 1, 5)]
  transfers between devices with their start and end apart: 4 -> 0, of which waited for: 1 -> 0; matrix products, arithmetic and copies ran while one was open for 18% -> 0% of each run, Pallas kernels for 16% -> 0%
where the time goes in v2:
time: 117 us; the launch traced here: 115 us
  Pallas kernels  104 us (89%)
  local copies, waits for them, and re-layouts  10.5 us (9%)
    pallas_call x1, Pallas kernels, on_device(): pl.pallas_call(functools.partial(whole_kernel, lax.axis_size('seq')), out...  104 us
    unnamed x10, local copies, waits for them, and re-layouts  5.24 us

profile of v2, /device:TPU:1, one launch (start us, length us, event | category | flops | bytes accessed | tf_op | source)
XLA Modules:
  0.0 115.4 jit_solution(16260523578329663161)
XLA Ops:
  0.6 1.3 %reshape.21.lng_ref = f32[1,1536]{1,0:T(1,128)} reshape(f32[1536]{0:T(1024)} %param.9) | data formatting | bytes 12288 | tf_op jit(solution)/shard_map/reshape | solution.py:813
  1.9 1.3 %reshape.22.bng_ref = f32[1,1536]{1,0:T(1,128)} reshape(f32[1536]{0:T(1024)} %param.12) | data formatting | bytes 12288 | tf_op jit(solution)/shard_map/reshape | solution.py:816
  3.2 1.3 %reshape.23.bnb_ref = f32[1,1536]{1,0:T(1,128)} reshape(f32[1536]{0:T(1024)} %param.13) | data formatting | bytes 12288 | tf_op jit(solution)/shard_map/reshape | solution.py:817
  4.5 104.2 %shard_map.127 = (bf16[2,256,1536]{2,1,0:T(8,128)(2,1)}, bf16[2,256,1536]{2,1,0:T(8,128)(2,1)}, f32[12,1536]{1,0:T(8,128)}, f32[32,1536]{1,0:T(8,128)}, f32[2,1536]{1,0:T(2,128)}) custom-call(bf16[2,256,1536]{2,1,0:T(8,128)(2,1)} %x_hbm.1, f32[1,1536]{1,0:T(1,128)} %reshape.21.lng_ref, bf16[1536,3072]{1,0:T(8,128)(2,1)} %win_hbm.1, f32[32,1536]{1,0:T(8,128)} %ker_ref.1, ...), custom_call_target="tpu_custom_call" | custom-call | tf_op jit(solution)/shard_map/pallas_call | solution.py:796
  108.8 1.4 %slice_reduce_fusion = (f32[1536]{0:T(1024)}, f32[1536]{0:T(1024)}) fusion(f32[2,1536]{1,0:T(2,128)} %get-tuple-element.15), kind=kLoop, calls=%fused_computation | loop fusion | bytes 24576 | tf_op jit(solution)/shard_map/slice | solution.py:821
  110.2 0.0 copy-start
  110.2 2.8 %copy.18 = bf16[2,256,1536]{2,1,0:T(8,128)(2,1)} copy(bf16[2,256,1536]{2,1,0:T(8,128)(2,1)} %get-tuple-element.24) | data formatting | bytes 3145728
  112.9 0.0 copy-done
  112.9 0.0 copy-start.2
  112.9 0.0 copy-start.1
  113.0 1.1 copy.19
  114.1 0.0 copy-done.2
  114.1 0.6 copy.20
  114.7 0.0 copy-done.1
  114.7 0.7 copy.21
Async XLA Ops:
  110.2 2.8 %copy-start = (bf16[2,256,1536]{2,1,0:T(8,128)(2,1)S(1)}, bf16[2,256,1536]{2,1,0:T(8,128)(2,1)}, u32[]{:S(2)}) copy-start(bf16[2,256,1536]{2,1,0:T(8,128)(2,1)} %get-tuple-element.25) | copy-start | bytes 4718596
  112.9 1.1 copy-start.2
  112.9 1.8 %copy-start.1 = (f32[32,1536]{1,0:T(8,128)S(1)}, f32[32,1536]{1,0:T(8,128)}, u32[]{:S(2)}) copy-start(f32[32,1536]{1,0:T(8,128)} %get-tuple-element.27) | copy-start | bytes 589828

commit v3 on v2

--- a/solution.py
+++ b/solution.py
@@ -403,23 +403,32 @@
     s = dict(zip([name for name, _ in SCRATCH], scratch))
     me = lax.axis_index("seq")
     local = s["local_sem"]
-    loads = [
-        pltpu.make_async_copy(x_hbm, s["x_raw"], local.at[0]),
-        pltpu.make_async_copy(win_hbm, s["w_in"], local.at[1]),
-        pltpu.make_async_copy(cot_hbm, s["cot_raw"], local.at[2]),
-        pltpu.make_async_copy(wout_hbm, s["w_out"], local.at[3]),
-    ]
-    for load in loads:
-        load.start()
+    load_x = [pltpu.make_async_copy(x_hbm.at[u], s["x_raw"].at[u], local.at[u]) for u in range(UTT)]
+    load_cot = pltpu.make_async_copy(cot_hbm, s["cot_raw"], local.at[2])
+    load_out = pltpu.make_async_copy(wout_hbm, s["w_out"], local.at[3])
+
+    def load_in(c):
+        found = []
+        for side in range(2):
+            cols = pl.ds(pl.multiple_of(side * D + c * CHUNK, CHUNK), CHUNK)
+            found.append(
+                pltpu.make_async_copy(win_hbm.at[:, cols], s["w_in"].at[:, cols], s["win_sem"].at[c, side])
+            )
+        return found
+
+    for copy in load_x + load_in(0):
+        copy.start()
+    vec = s["vec"]
+    for row, ref in enumerate((lng_ref, bng_ref, bnb_ref)):
+        vec[row : row + 1, :] = ref[...].reshape(1, D)
     net = Net(me, s["send_sem"], s["recv_sem"])
     halo1 = Halo(me, n_dev, s["h_out1"], s["h_got1"], s["h_send1"], s["h_recv1"])
     halo2 = Halo(me, n_dev, s["h_out2"], s["h_got2"], s["h_send2"], s["h_recv2"])
 
-    perm, perm_t, eye, select = s["perm"], s["perm_t"], s["eye"], s["select"]
+    perm, eye, select = s["perm"], s["eye"], s["select"]
     r0 = lax.broadcasted_iota(jnp.int32, (256, 256), 0)
     r1 = lax.broadcasted_iota(jnp.int32, (256, 256), 1)
     perm[...] = jnp.where(frame_of(r0) == r1, 1.0, 0.0).astype(BF16)
-    perm_t[...] = jnp.where(frame_of(r1) == r0, 1.0, 0.0).astype(BF16)
     eye[...] = jnp.where(r0 == r1, 1.0, 0.0).astype(BF16)
     q0 = lax.broadcasted_iota(jnp.int32, (32, 256), 0)
     q1 = lax.broadcasted_iota(jnp.int32, (32, 256), 1)
@@ -428,7 +437,11 @@
     row_id = lax.broadcasted_iota(jnp.int32, (8, 128), 0)
 
     x_p, normed, mu_ref, rstd_ref = s["x_p"], s["bf"], s["mu"], s["rstd"]
-    loads[0].wait()
+    for copy in load_x:
+        copy.wait()
+    for c in range(1, CHUNKS):
+        for copy in load_in(c):
+            copy.start()
 
     def norm_tile(i, carry):
         u, part = i // 4, lax.rem(i, 4)
@@ -440,16 +453,17 @@
         rstd = lax.rsqrt(jnp.mean(gap * gap, axis=-1, keepdims=True) + EPSILON)
         mu_ref[rows, :] = mean
         rstd_ref[rows, :] = rstd
-        normed[rows, :] = (gap * rstd * lng_ref[...]).astype(BF16)
+        normed[rows, :] = (gap * rstd * vec[0:1, :]).astype(BF16)
         return carry
 
     lax.fori_loop(0, 8, norm_tile, 0)
     greet(me, AXES, (halo1.left, halo1.right))
-    loads[1].wait()
     w_in, val, gs, ext_g, ext_d = s["w_in"], s["val"], s["gs"], s["ext_g"], s["ext_d"]
 
     def project(c, carry):
         cols = span(c, CHUNK)
+        for copy in load_in(c):
+            copy.wait()
         val[:, cols] = dot(normed[...], w_in[:, cols])
         gate_cols = pl.ds(pl.multiple_of(D + c * CHUNK, CHUNK), CHUNK)
         gs[:, cols] = dot(normed[...], w_in[:, gate_cols])
@@ -465,6 +479,8 @@
         return carry
 
     lax.fori_loop(0, CHUNKS, project, 0)
+    load_cot.start()
+    load_out.start()
 
     def halo_rows(halo, c, u, lane):
         low = halo.got[c, 0, u, :, lane : lane + 128].astype(F32)
@@ -499,7 +515,7 @@
 
     ar1 = Reduce(net, True, s["cur1"], s["ar1"])
     ar1.start(stat[...])
-    loads[2].wait()
+    load_cot.wait()
     cot_p, cot_t, w_out = s["cot_p"], s["cot_t"], s["w_out"]
 
     def turn(c, carry):
@@ -511,7 +527,7 @@
 
     lax.fori_loop(0, CHUNKS, turn, 0)
     ar1.step()
-    loads[3].wait()
+    load_out.wait()
 
     def act_grad(c, carry):
         cols = span(c, CHUNK)
@@ -534,7 +550,7 @@
     def bn_block(cb, carry):
         cols = span(cb, 128)
         mean, rstd = coef[0:1, cols], coef[1:2, cols]
-        gain, bias = bng_ref[:, cols], bnb_ref[:, cols]
+        gain, bias = vec[1:2, cols], vec[2:3, cols]
         sum_bias = jnp.zeros((8, 128), F32)
         sum_gain = jnp.zeros((8, 128), F32)
         for u in range(UTT):
@@ -563,15 +579,15 @@
     def weight_part(h, p):
         cols = pl.ds(pl.multiple_of(h * HALF + p * CHUNK, CHUNK), CHUNK)
 
-        def tile(m, carry):
-            res = dot(cot_t[span(m, 192), :], act[:, cols])
-            for j in range(8):
+        def weight_tile(m, carry):
+            res = dot(cot_t[span(m, 384), :], act[:, cols])
+            for j in range(16):
                 piece = res[j * 24 : j * 24 + 24]
                 piece = jnp.concatenate([piece[:, 0:128], piece[:, 128:256]], axis=0).astype(BF16)
-                part_ref[h, p, m // 2, lax.rem(m, 2) * 2 + j // 4, j % 4] = piece
+                part_ref[h, p, m, j // 4, j % 4] = piece
             return carry
 
-        lax.fori_loop(0, 8, tile, 0)
+        lax.fori_loop(0, 4, weight_tile, 0)
 
     firsts = []
     for p in range(3):
@@ -580,30 +596,24 @@
     ar2.step()
     saves = []
 
-    def branch(u):
-        rows = pl.ds(u * 256, 256)
-
-        def tile(n, carry):
-            cols = span(n, CHUNK)
-            res = dot_t(act[rows, :], w_out[cols, :])
-            res = (x_p[rows, cols].astype(F32) + res).astype(BF16)
-            s["x_raw"][u, :, cols] = dot(perm_t[...], res).astype(BF16)
-            return carry
-
-        lax.fori_loop(0, CHUNKS, tile, 0)
-        copy = pltpu.make_async_copy(s["x_raw"].at[u], out_hbm.at[u], local.at[4 + u])
-        copy.start()
-        saves.append(copy)
-
-    branch(0)
+    def branch(n, carry):
+        cols = span(n, CHUNK)
+        res = dot_t(act[...], w_out[cols, :])
+        s["out_p"][:, cols] = (x_p[:, cols].astype(F32) + res).astype(BF16)
+        return carry
+
+    lax.fori_loop(0, CHUNKS // 2, branch, 0)
     ar2.step()
-    branch(1)
+    lax.fori_loop(CHUNKS // 2, CHUNKS, branch, 0)
+    copy = pltpu.make_async_copy(s["out_p"], out_hbm, local.at[4])
+    copy.start()
+    saves.append(copy)
     ar2.step()
     for p in range(3):
         weight_part(core, p)
     sums = ar2.take()
     dbn_ref[...] = sums
-    gain_row = bng_ref[...]
+    gain_row = vec[1:2, :]
     rstd_row = coef[1:2, :]
     coef[2:3, :] = rstd_row * gain_row
     coef[3:4, :] = rstd_row * (gain_row * sums[1:2] * (1.0 / total_rows))
@@ -633,20 +643,25 @@
     def kernel_grad(h):
         def body(n, carry):
             cols = pl.ds(pl.multiple_of(h * HALF + n * 128, 128), 128)
-            acc = [jnp.zeros((8, 128), F32)] * K
-            for u in range(UTT):
-                for base in range(0, 32, 8):
-                    grads = [
-                        ext_d[u, OWN + (base + o) * 8 : OWN + (base + o) * 8 + 8, cols] for o in range(8)
-                    ]
-                    for e in range(base + 1, base + 40):
-                        x = ext_g[u, e * 8 : e * 8 + 8, cols]
-                        for o in range(8):
-                            k = e - (base + o) - 1
-                            if 0 <= k < K:
-                                acc[k] = acc[k] + x * grads[o]
-            for k in range(K):
-                dk_src[h, k // 8, k % 8 : k % 8 + 1, span(n, 128)] = jnp.sum(acc[k], axis=0, keepdims=True)
+            for first in range(0, K, 16):
+                acc = [jnp.zeros((8, 128), F32)] * 16
+                for u in range(UTT):
+                    for base in range(0, 32, 8):
+                        grads = [
+                            ext_d[u, OWN + (base + o) * 8 : OWN + (base + o) * 8 + 8, cols]
+                            for o in range(8)
+                        ]
+                        for e in range(base + first + 1, base + first + 24):
+                            x = ext_g[u, e * 8 : e * 8 + 8, cols]
+                            for o in range(8):
+                                k = e - (base + o) - 1 - first
+                                if 0 <= k < 16:
+                                    acc[k] = acc[k] + x * grads[o]
+                for a in range(16):
+                    k = first + a
+                    dk_src[h, k // 8, k % 8 : k % 8 + 1, span(n, 128)] = jnp.sum(
+                        acc[a], axis=0, keepdims=True
+                    )
             return carry
 
         lax.fori_loop(0, HALF // 128, body, 0)
@@ -705,7 +720,7 @@
     def norm_grad(u):
         def tile(i, carry):
             rows = pl.ds(pl.multiple_of(u * 256 + i * 32, 32), 32)
-            d_hat = conv[rows, :] * lng_ref[...]
+            d_hat = conv[rows, :] * vec[0:1, :]
             rstd = rstd_ref[rows, :]
             hat = (x_p[rows, :].astype(F32) - mu_ref[rows, :]) * rstd
             m1 = jnp.mean(d_hat, axis=-1, keepdims=True)
@@ -716,13 +731,8 @@
 
         lax.fori_loop(0, 8, tile, 0)
 
-        def back(n, carry):
-            cols = span(n, CHUNK)
-            s["cot_raw"][u, :, cols] = dot(perm_t[...], act[u * 256 : u * 256 + 256, cols]).astype(BF16)
-            return carry
-
-        lax.fori_loop(0, CHUNKS, back, 0)
-        copy = pltpu.make_async_copy(s["cot_raw"].at[u], din_hbm.at[u], local.at[6 + u])
+        rows_u = pl.ds(u * 256, 256)
+        copy = pltpu.make_async_copy(act.at[rows_u], din_hbm.at[rows_u], local.at[6 + u])
         copy.start()
         saves.append(copy)
 
@@ -750,7 +760,9 @@
     ("cot_raw", VM((UTT, 256, D), BF16)),
     ("w_out", VM((D, D), BF16)),
     ("perm", VM((256, 256), BF16)),
-    ("perm_t", VM((256, 256), BF16)),
+    ("win_sem", pltpu.SemaphoreType.DMA((CHUNKS, 2))),
+    ("vec", VM((3, D), F32)),
+    ("out_p", VM((ROWS, D), BF16)),
     ("eye", VM((256, 256), BF16)),
     ("select", VM((32, 256), BF16)),
     ("x_p", VM((ROWS, D), BF16)),
@@ -790,14 +802,30 @@
 ]
 
 
+def finish_kernel(out_p, din_p, dw, dk, dbn, out_ref, din_ref, dw_out, dk_out, gain_out, bias_out, perm_t):
+    @pl.when((pl.program_id(0) == 0) & (pl.program_id(1) == 0))
+    def _():
+        r0 = lax.broadcasted_iota(jnp.int32, (256, 256), 0)
+        r1 = lax.broadcasted_iota(jnp.int32, (256, 256), 1)
+        perm_t[...] = jnp.where(frame_of(r1) == r0, 1.0, 0.0).astype(BF16)
+        dw_out[...] = dw[...]
+        dk_out[...] = dk[...]
+        gain_out[...] = dbn[0:1, :].reshape(D)
+        bias_out[...] = dbn[1:2, :].reshape(D)
+
+    out_ref[0] = dot(perm_t[...], out_p[...]).astype(BF16)
+    din_ref[0] = dot(perm_t[...], din_p[...]).astype(BF16)
+
+
 def on_device(inputs, ln_gain, w_in, kernel, bn_gain, bn_bias, w_out, cotangent):
     any_spec = pl.BlockSpec(memory_space=pl.ANY)
     vmem_spec = pl.BlockSpec(memory_space=pltpu.VMEM)
-    outputs, d_inputs, d_w_out, d_kernel, d_bn = pl.pallas_call(
+    flat = jax.ShapeDtypeStruct((ROWS, D), BF16)
+    out_p, din_p, dw, dk, dbn = pl.pallas_call(
         functools.partial(whole_kernel, lax.axis_size("seq")),
         out_shape=(
-            jax.ShapeDtypeStruct((UTT, FRAMES_DEV, D), BF16),
-            jax.ShapeDtypeStruct((UTT, FRAMES_DEV, D), BF16),
+            flat,
+            flat,
             jax.ShapeDtypeStruct((D // 128, D), F32),
             jax.ShapeDtypeStruct((K, D), F32),
             jax.ShapeDtypeStruct((2, D), F32),
@@ -808,17 +836,30 @@
         compiler_params=pltpu.CompilerParams(
             collective_id=0, has_side_effects=True, vmem_limit_bytes=67043328
         ),
-    )(
-        inputs,
-        ln_gain.reshape(1, D),
-        w_in,
-        kernel,
-        bn_gain.reshape(1, D),
-        bn_bias.reshape(1, D),
-        w_out,
-        cotangent,
-    )
-    return (outputs, d_inputs, d_w_out, d_kernel, d_bn[0], d_bn[1])
+    )(inputs, ln_gain, w_in, kernel, bn_gain, bn_bias, w_out, cotangent)
+
+    def whole(shape):
+        return pl.BlockSpec(shape, lambda u, c: (0,) * len(shape))
+
+    wide = D // 2
+    rows_spec = pl.BlockSpec((256, wide), lambda u, c: (u, c))
+    block_spec = pl.BlockSpec((1, 256, wide), lambda u, c: (u, 0, c))
+    full = jax.ShapeDtypeStruct((UTT, FRAMES_DEV, D), BF16)
+    return pl.pallas_call(
+        finish_kernel,
+        grid=(UTT, 2),
+        out_shape=(
+            full,
+            full,
+            jax.ShapeDtypeStruct((D // 128, D), F32),
+            jax.ShapeDtypeStruct((K, D), F32),
+            jax.ShapeDtypeStruct((D,), F32),
+            jax.ShapeDtypeStruct((D,), F32),
+        ),
+        in_specs=[rows_spec, rows_spec, whole((D // 128, D)), whole((K, D)), whole((2, D))],
+        out_specs=[block_spec, block_spec, whole((D // 128, D)), whole((K, D)), whole((D,)), whole((D,))],
+        scratch_shapes=[pltpu.VMEM((256, 256), BF16)],
+    )(out_p, din_p, dw, dk, dbn)
 
 
 def solution(mesh):

time: 117 us -> 106 us (0.906)
  local copies, waits for them, and re-layouts: 10.5 us -> 0 us
    unnamed x10 -> x0, local copies, waits for them, and re-layouts: 5.24 us -> none
    pallas_call x1, Pallas kernels: 104 us -> 99.3 us  [on_device(): pl.pallas_call(functools.partial(whole_kernel, lax.axis_size('seq')), out...]
    pallas_call x0 -> x1, Pallas kernels: none -> 4.82 us  [on_device(): pl.pallas_call(finish_kernel, grid=(UTT, 2), out_shape=(full, full, jax.S...]
    reshape x3 -> x0, local copies, waits for them, and re-layouts: 3.88 us -> none  [the longest x1 1.3 us: on_device(): ln_gain.reshape(1, D)]
    slice x1 -> x0, local copies, waits for them, and re-layouts: 1.42 us -> none  [on_device(): return (outputs, d_inputs, d_w_out, d_kernel, d_bn[0], d_bn[1])]
where the time goes in v3:
time: 106 us; the launch traced here: 105 us
  Pallas kernels  104 us (98%)
    pallas_call x1, Pallas kernels, on_device(): pl.pallas_call(functools.partial(whole_kernel, lax.axis_size('seq')), out...  99.3 us
    pallas_call x1, Pallas kernels, on_device(): pl.pallas_call(finish_kernel, grid=(UTT, 2), out_shape=(full, full, jax.S...  4.82 us

profile of v3, /device:TPU:1, one launch (start us, length us, event | category | flops | bytes accessed | tf_op | source)
XLA Modules:
  0.0 104.8 jit_solution(1447529522012538821)
XLA Ops:
  0.6 99.3 %shard_map.127 = (bf16[512,1536]{1,0:T(8,128)(2,1)}, bf16[512,1536]{1,0:T(8,128)(2,1)}, f32[12,1536]{1,0:T(8,128)}, f32[32,1536]{1,0:T(8,128)}, f32[2,1536]{1,0:T(2,128)}) custom-call(bf16[2,256,1536]{2,1,0:T(8,128)(2,1)} %x_hbm.1, f32[1536]{0:T(1024)} %lng_ref.1, bf16[1536,3072]{1,0:T(8,128)(2,1)} %win_hbm.1, f32[32,1536]{1,0:T(8,128)} %ker_ref.1, ...), custom_call_target="tpu_custom_call" | custom-call | tf_op jit(solution)/shard_map/pallas_call | solution.py:824
  100.0 4.8 %shard_map.128 = (bf16[2,256,1536]{2,1,0:T(8,128)(2,1)}, bf16[2,256,1536]{2,1,0:T(8,128)(2,1)}, f32[12,1536]{1,0:T(8,128)}, f32[32,1536]{1,0:T(8,128)}, f32[1536]{0:T(1024)}, /*index=5*/f32[1536]{0:T(1024)}) custom-call(bf16[512,1536]{1,0:T(8,128)(2,1)} %get-tuple-element.11.out_p, bf16[512,1536]{1,0:T(8,128)(2,1)} %get-tuple-element.12.din_p, ...), custom_call_target="tpu_custom_call" | custom-call | tf_op jit(solution)/shard_map/pallas_call | solution.py:848

commit v4 on v3

--- a/solution.py
+++ b/solution.py
@@ -71,7 +71,7 @@
             barrier, inc=1, device_id=(device,), device_id_type=pl.DeviceIdType.MESH
         )
         count += 1
-    pl.semaphore_wait(barrier, count)
+    return lambda: pl.semaphore_wait(barrier, count)
 
 
 AXES = ("core", "z", "y", "x")
@@ -212,7 +212,7 @@
             self.s[0][part, x, y] = (mine + theirs).astype(BF16)
             return carry
 
-        lax.fori_loop(0, 16, body, 0)
+        lax.fori_loop(0, 16, body, 0, unroll=2)
 
     def send_level(self, part, level):
         me = self.net.me
@@ -384,18 +384,29 @@
         ext[u, (48 + j) * 8 : (49 + j) * 8, cols] = jnp.where(row_id == 7, high[j : j + 1], above)
 
 
-def convolve(ext, u, cols, taps, forward):
-    for base in range(0, 32, 8):
-        acc = [None] * 8
-        reach = range(base + 1, base + 40) if forward else range(base, base + 39)
-        for e in reach:
-            x = ext[u, e * 8 : e * 8 + 8, cols]
-            for o in range(8):
-                k = e - (base + o) - 1 if forward else base + o + 31 - e
-                if 0 <= k < K:
-                    term = taps[k] * x
-                    acc[o] = term if acc[o] is None else acc[o] + term
-        yield base, acc
+def convolve(ext, u, cols, taps, offset):
+    low, high = taps[0::2], taps[1::2]
+    both = [a + b for a, b in zip(low, high)]
+
+    def x(n):
+        return ext[u, (n + offset) * 8 : (n + offset) * 8 + 8, cols]
+
+    def product(weights, source, start, first):
+        acc = list(start)
+        for n in range(first, first + 23):
+            value = source(n)
+            for p in range(8):
+                m = n - first - p
+                if 0 <= m < 16:
+                    term = weights[m] * value
+                    acc[p] = term if acc[p] is None else acc[p] + term
+        return acc
+
+    for first in (0, 8):
+        shared = product(both, lambda n: x(2 * n + 1), [None] * 8, first)
+        even = product(low, lambda n: x(2 * n) - x(2 * n + 1), shared, first)
+        odd = product(high, lambda n: x(2 * n + 2) - x(2 * n + 1), shared, first)
+        yield 2 * first, [v for pair in zip(even, odd) for v in pair]
 
 
 def whole_kernel(n_dev, x_hbm, lng_ref, win_hbm, ker_ref, bng_ref, bnb_ref, wout_hbm, cot_hbm,
@@ -425,6 +436,7 @@
     halo1 = Halo(me, n_dev, s["h_out1"], s["h_got1"], s["h_send1"], s["h_recv1"])
     halo2 = Halo(me, n_dev, s["h_out2"], s["h_got2"], s["h_send2"], s["h_recv2"])
 
+    entered = greet(me, AXES, (halo1.left, halo1.right))
     perm, eye, select = s["perm"], s["eye"], s["select"]
     r0 = lax.broadcasted_iota(jnp.int32, (256, 256), 0)
     r1 = lax.broadcasted_iota(jnp.int32, (256, 256), 1)
@@ -443,11 +455,17 @@
         for copy in load_in(c):
             copy.start()
 
+    def permute(c, carry):
+        cols = span(c, CHUNK)
+        for u in range(UTT):
+            x_p[u * 256 : u * 256 + 256, cols] = dot(perm[...], s["x_raw"][u, :, cols]).astype(BF16)
+        return carry
+
+    lax.fori_loop(0, CHUNKS, permute, 0)
+
     def norm_tile(i, carry):
-        u, part = i // 4, lax.rem(i, 4)
-        rows = span(i, 64)
-        x = dot(perm[span(part, 64), :], s["x_raw"][u])
-        x_p[rows, :] = x.astype(BF16)
+        rows = span(i, 16)
+        x = x_p[rows, :].astype(F32)
         mean = jnp.mean(x, axis=-1, keepdims=True)
         gap = x - mean
         rstd = lax.rsqrt(jnp.mean(gap * gap, axis=-1, keepdims=True) + EPSILON)
@@ -456,14 +474,18 @@
         normed[rows, :] = (gap * rstd * vec[0:1, :]).astype(BF16)
         return carry
 
-    lax.fori_loop(0, 8, norm_tile, 0)
-    greet(me, AXES, (halo1.left, halo1.right))
+    lax.fori_loop(0, ROWS // 16, norm_tile, 0, unroll=4)
+    entered()
     w_in, val, gs, ext_g, ext_d = s["w_in"], s["val"], s["gs"], s["ext_g"], s["ext_d"]
 
     def project(c, carry):
-        cols = span(c, CHUNK)
         for copy in load_in(c):
             copy.wait()
+        project_chunk(c)
+        return carry
+
+    def project_chunk(c):
+        cols = span(c, CHUNK)
         val[:, cols] = dot(normed[...], w_in[:, cols])
         gate_cols = pl.ds(pl.multiple_of(D + c * CHUNK, CHUNK), CHUNK)
         gs[:, cols] = dot(normed[...], w_in[:, gate_cols])
@@ -476,7 +498,6 @@
             ext_g[u, OWN : OWN + 256, cols] = gated.astype(F32)
             blocks.append(gated)
         halo1.push(c, select, blocks)
-        return carry
 
     lax.fori_loop(0, CHUNKS, project, 0)
     load_cot.start()
@@ -492,8 +513,12 @@
     def taps_of(cols):
         return [jnp.broadcast_to(ker_ref[k : k + 1, cols], (8, 128)) for k in range(K)]
 
-    def conv_chunk(c, carry):
+    def conv_only(c, carry):
         halo1.wait(c)
+        conv_chunk(c)
+        return carry
+
+    def conv_chunk(c):
         for half in range(2):
             cols = pl.ds(pl.multiple_of(c * CHUNK + half * 128, 128), 128)
             taps = taps_of(cols)
@@ -501,20 +526,25 @@
             for u in range(UTT):
                 low, high = halo_rows(halo1, c, u, half * 128)
                 extend(ext_g, u, cols, low, high, row_id)
-                for base, acc in convolve(ext_g, u, cols, taps, True):
-                    for o in range(8):
+                for base, acc in convolve(ext_g, u, cols, taps, 1):
+                    for o in range(16):
                         conv[pl.ds(u * 256 + (base + o) * 8, 8), cols] = acc[o]
                         total = total + acc[o]
             mean = jnp.sum(total, axis=0, keepdims=True) * (1.0 / ROWS)
             gap = conv[:, cols] - mean
             stat[0:1, cols] = mean
             stat[1:2, cols] = jnp.sum(fold(gap * gap), axis=0, keepdims=True)
-        return carry
-
-    lax.fori_loop(0, CHUNKS, conv_chunk, 0)
-
-    ar1 = Reduce(net, True, s["cur1"], s["ar1"])
-    ar1.start(stat[...])
+
+    wide = (slice(0, HALF), slice(HALF, D))
+    ar1 = [Reduce(net, True, s["cur"].at[h], s["got"].at[h]) for h in range(2)]
+    ar2 = [Reduce(net, False, s["cur"].at[2 + h], s["got"].at[2 + h]) for h in range(2)]
+    lax.fori_loop(0, 3, conv_only, 0)
+    ar1[0].start(stat[:, wide[0]])
+    lax.fori_loop(3, 4, conv_only, 0)
+    ar1[0].step()
+    lax.fori_loop(4, CHUNKS, conv_only, 0)
+    ar1[0].step()
+    ar1[1].start(stat[:, wide[1]])
     load_cot.wait()
     cot_p, cot_t, w_out = s["cot_p"], s["cot_t"], s["w_out"]
 
@@ -525,8 +555,9 @@
         cot_t[cols, :] = dot_t(eye[...], cot_p[:, cols]).astype(BF16)
         return carry
 
-    lax.fori_loop(0, CHUNKS, turn, 0)
-    ar1.step()
+    lax.fori_loop(0, CHUNKS, turn, 0, unroll=2)
+    ar1[1].step()
+    ar1[0].step()
     load_out.wait()
 
     def act_grad(c, carry):
@@ -536,15 +567,18 @@
             ext_d[u, OWN : OWN + 256, cols] = res[u * 256 : u * 256 + 256]
         return carry
 
-    lax.fori_loop(0, CHUNKS // 2, act_grad, 0)
-    ar1.step()
-    lax.fori_loop(CHUNKS // 2, CHUNKS, act_grad, 0)
-    ar1.step()
-    stats = ar1.take()
     total_rows = float(ROWS * n_dev)
     coef = s["coef"]
-    coef[0:1, :] = stats[0:1]
-    coef[1:2, :] = lax.rsqrt(stats[1:2] * (1.0 / total_rows) + EPSILON)
+
+    def use_stats(h):
+        stats = ar1[h].take()
+        coef[0:1, wide[h]] = stats[0:1]
+        coef[1:2, wide[h]] = lax.rsqrt(stats[1:2] * (1.0 / total_rows) + EPSILON)
+
+    lax.fori_loop(0, CHUNKS // 2, act_grad, 0)
+    ar1[1].step()
+    lax.fori_loop(CHUNKS // 2, CHUNKS, act_grad, 0)
+    use_stats(0)
     act = s["bf"]
 
     def bn_block(cb, carry):
@@ -568,10 +602,6 @@
         stat[1:2, cols] = jnp.sum(sum_bias, axis=0, keepdims=True)
         return carry
 
-    lax.fori_loop(0, D // 128, bn_block, 0)
-    ar2 = Reduce(net, False, s["cur2"], s["ar2"])
-    ar2.start(stat[...])
-
     core = coord(me, "core")
     part_ref = s["part"]
     rs = Scatter(net, part_ref, *[s[name] for name in RS_NAMES])
@@ -587,13 +617,8 @@
                 part_ref[h, p, m, j // 4, j % 4] = piece
             return carry
 
-        lax.fori_loop(0, 4, weight_tile, 0)
-
-    firsts = []
-    for p in range(3):
-        weight_part(1 - core, p)
-        firsts.append(rs.start(p))
-    ar2.step()
+        lax.fori_loop(0, 4, weight_tile, 0, unroll=2)
+
     saves = []
 
     def branch(n, carry):
@@ -602,22 +627,39 @@
         s["out_p"][:, cols] = (x_p[:, cols].astype(F32) + res).astype(BF16)
         return carry
 
+    def use_sums(h):
+        sums = ar2[h].take()
+        dbn_ref[:, wide[h]] = sums
+        gain_row = vec[1:2, wide[h]]
+        rstd_row = coef[1:2, wide[h]]
+        coef[2:3, wide[h]] = rstd_row * gain_row
+        coef[3:4, wide[h]] = rstd_row * (gain_row * sums[1:2] * (1.0 / total_rows))
+        coef[4:5, wide[h]] = rstd_row * (gain_row * sums[0:1] * (1.0 / total_rows))
+
+    lax.fori_loop(0, 6, bn_block, 0)
+    ar1[1].step()
+    ar2[0].start(stat[:, wide[0]])
+    weight_part(0, 0)
+    weight_part(0, 1)
+    ar2[0].step()
+    weight_part(0, 2)
+    use_stats(1)
+    lax.fori_loop(6, 12, bn_block, 0)
+    ar2[0].step()
+    ar2[1].start(stat[:, wide[1]])
+    weight_part(1, 0)
+    weight_part(1, 1)
+    ar2[1].step()
+    weight_part(1, 2)
     lax.fori_loop(0, CHUNKS // 2, branch, 0)
-    ar2.step()
+    ar2[0].step()
+    ar2[1].step()
+    firsts = [rs.start(p) for p in range(3)]
     lax.fori_loop(CHUNKS // 2, CHUNKS, branch, 0)
     copy = pltpu.make_async_copy(s["out_p"], out_hbm, local.at[4])
     copy.start()
     saves.append(copy)
-    ar2.step()
-    for p in range(3):
-        weight_part(core, p)
-    sums = ar2.take()
-    dbn_ref[...] = sums
-    gain_row = vec[1:2, :]
-    rstd_row = coef[1:2, :]
-    coef[2:3, :] = rstd_row * gain_row
-    coef[3:4, :] = rstd_row * (gain_row * sums[1:2] * (1.0 / total_rows))
-    coef[4:5, :] = rstd_row * (gain_row * sums[0:1] * (1.0 / total_rows))
+    use_sums(0)
 
     def conv_grad(c, carry):
         cols = span(c, CHUNK)
@@ -627,99 +669,111 @@
             xhat = conv[u * 256 : u * 256 + 256, cols]
             d_conv = d_bn * coef[2:3, cols] - coef[3:4, cols] - xhat * coef[4:5, cols]
             ext_d[u, OWN : OWN + 256, cols] = d_conv
+            conv[u * 256 : u * 256 + 256, cols] = jnp.zeros((256, CHUNK), F32)
             blocks.append(d_conv.astype(BF16))
         halo2.push(c, select, blocks)
         return carry
 
-    lax.fori_loop(0, CHUNKS, conv_grad, 0)
+    dk_src = s["dk_src"]
+
+    def kernel_grad(h):
+        def tap_sums(n, carry):
+            cols = pl.ds(pl.multiple_of(h * HALF + n * 128, 128), 128)
+            for u in range(UTT):
+                grads = [ext_d[u, OWN + i * 8 : OWN + i * 8 + 8, cols] for i in range(32)]
+                for base, acc in convolve(ext_g, u, cols, grads, 1):
+                    for part in range(2):
+                        row = base // 8 + part
+                        folded = jnp.concatenate(
+                            [jnp.sum(a, axis=0, keepdims=True) for a in acc[part * 8 : part * 8 + 8]],
+                            axis=0,
+                        )
+                        if u == 0:
+                            dk_src[h, row, :, span(n, 128)] = folded
+                        else:
+                            dk_src[h, row, :, span(n, 128)] += folded
+            return carry
+
+        lax.fori_loop(0, HALF // 128, tap_sums, 0)
+
+    lax.fori_loop(0, 3, conv_grad, 0)
+    ar2[1].step()
+    kernel_grad(0)
+    use_sums(1)
+    lax.fori_loop(3, CHUNKS, conv_grad, 0)
 
     levels = []
     for p in range(3):
         rs.add_core(p, firsts[p])
         levels.append(rs.send_level(p, 0))
 
-    dk_src = s["dk_src"]
-
-    def kernel_grad(h):
-        def body(n, carry):
-            cols = pl.ds(pl.multiple_of(h * HALF + n * 128, 128), 128)
-            for first in range(0, K, 16):
-                acc = [jnp.zeros((8, 128), F32)] * 16
-                for u in range(UTT):
-                    for base in range(0, 32, 8):
-                        grads = [
-                            ext_d[u, OWN + (base + o) * 8 : OWN + (base + o) * 8 + 8, cols]
-                            for o in range(8)
-                        ]
-                        for e in range(base + first + 1, base + first + 24):
-                            x = ext_g[u, e * 8 : e * 8 + 8, cols]
-                            for o in range(8):
-                                k = e - (base + o) - 1 - first
-                                if 0 <= k < 16:
-                                    acc[k] = acc[k] + x * grads[o]
-                for a in range(16):
-                    k = first + a
-                    dk_src[h, k // 8, k % 8 : k % 8 + 1, span(n, 128)] = jnp.sum(
-                        acc[a], axis=0, keepdims=True
-                    )
-            return carry
-
-        lax.fori_loop(0, HALF // 128, body, 0)
-
     dk = DKernel(net, dk_src, *[s[name] for name in DK_NAMES])
-    kernel_grad(1 - core)
+    kernel_grad(1)
     dk.start()
+    grads = (s["d_proj0"], s["d_proj1"])
+
+    def input_grad(c, d_proj):
+        halo2.wait(c)
+        for half in range(2):
+            start = pl.multiple_of(c * CHUNK + half * 128, 128)
+            cols = pl.ds(start, 128)
+            taps = taps_of(cols)[::-1]
+            lane = half * 128
+            for u in range(UTT):
+                low, high = halo_rows(halo2, c, u, lane)
+                extend(ext_d, u, cols, low, high, row_id)
+                for base, acc in convolve(ext_d, u, cols, taps, 0):
+                    rows = pl.ds(u * 256 + base * 8, 128)
+                    grad = jnp.concatenate(acc, axis=0)
+                    sig = gs[rows, cols]
+                    by_sig = grad * sig
+                    d_proj[rows, lane : lane + 128] = by_sig.astype(BF16)
+                    d_proj[rows, CHUNK + lane : CHUNK + lane + 128] = (
+                        by_sig * val[rows, cols] * (1.0 - sig)
+                    ).astype(BF16)
+
+    def frame_grad(c, d_proj):
+        cols = span(c, CHUNK)
+        gate_cols = pl.ds(pl.multiple_of(D + c * CHUNK, CHUNK), CHUNK)
+        for n in range(CHUNKS):
+            rows = slice(n * CHUNK, n * CHUNK + CHUNK)
+            weights = jnp.concatenate([w_in[rows, cols], w_in[rows, gate_cols]], axis=1)
+            conv[:, rows] += dot_t(d_proj[...], weights)
+
+    def both(j, carry):
+        for odd in range(2):
+            c = 2 * j + odd
+            input_grad(c + 1, grads[1 - odd])
+            frame_grad(c, grads[odd])
+        return carry
+
+    input_grad(0, grads[0])
+    lax.fori_loop(0, 1, both, 0)
+    dk.to_x()
     nexts = []
     for p in range(3):
         rs.add_level(p, 0, levels[p])
         nexts.append(rs.send_level(p, 1))
-    kernel_grad(core)
-    dk.to_x()
-    d_proj = s["d_proj"]
-
-    def input_grad(c, carry):
-        halo2.wait(c)
-        for half in range(2):
-            start = pl.multiple_of(c * CHUNK + half * 128, 128)
-            cols = pl.ds(start, 128)
-            gate_cols = pl.ds(pl.multiple_of(D + start, 128), 128)
-            taps = taps_of(cols)
-            for u in range(UTT):
-                low, high = halo_rows(halo2, c, u, half * 128)
-                extend(ext_d, u, cols, low, high, row_id)
-                for base, acc in convolve(ext_d, u, cols, taps, False):
-                    rows = pl.ds(u * 256 + base * 8, 64)
-                    grad = jnp.concatenate(acc, axis=0)
-                    sig = gs[rows, cols]
-                    by_sig = grad * sig
-                    d_proj[rows, cols] = by_sig.astype(BF16)
-                    d_proj[rows, gate_cols] = (by_sig * val[rows, cols] * (1.0 - sig)).astype(BF16)
-        return carry
-
-    lax.fori_loop(0, CHUNKS // 2, input_grad, 0)
+    lax.fori_loop(1, 2, both, 0)
+    dk.to_z()
     levels = nexts
     nexts = []
     for p in range(3):
         rs.add_level(p, 1, levels[p])
         nexts.append(rs.send_level(p, 2))
-    dk.to_z()
-    lax.fori_loop(CHUNKS // 2, CHUNKS, input_grad, 0)
+    input_grad(5, grads[1])
+    dk.to_y()
+    frame_grad(4, grads[0])
+    halo1.drain()
+    halo2.drain()
     rs.exchange([rs.add_level(p, 2, nexts[p]) for p in range(3)])
-    dk.to_y()
-
-    def frame_grad(u):
-        rows_u = pl.ds(u * 256, 256)
-
-        def tile(n, carry):
-            cols = span(n, CHUNK)
-            conv[rows_u, cols] = dot_t(d_proj[rows_u, :], w_in[cols, :])
-            return carry
-
-        lax.fori_loop(0, CHUNKS, tile, 0)
+    dk.gather_x()
+    frame_grad(5, grads[1])
+    dk.gather_core()
 
     def norm_grad(u):
         def tile(i, carry):
-            rows = pl.ds(pl.multiple_of(u * 256 + i * 32, 32), 32)
+            rows = pl.ds(pl.multiple_of(u * 128 + i * 16, 16), 16)
             d_hat = conv[rows, :] * vec[0:1, :]
             rstd = rstd_ref[rows, :]
             hat = (x_p[rows, :].astype(F32) - mu_ref[rows, :]) * rstd
@@ -729,26 +783,21 @@
             act[rows, :] = (cot_p[rows, :].astype(F32) + grad).astype(BF16)
             return carry
 
-        lax.fori_loop(0, 8, tile, 0)
-
-        rows_u = pl.ds(u * 256, 256)
+        lax.fori_loop(0, 8, tile, 0, unroll=4)
+        rows_u = pl.ds(u * 128, 128)
         copy = pltpu.make_async_copy(act.at[rows_u], din_hbm.at[rows_u], local.at[6 + u])
         copy.start()
         saves.append(copy)
 
-    frame_grad(0)
-    dk.gather_x()
     norm_grad(0)
-    dk.gather_core()
-    frame_grad(1)
+    norm_grad(1)
+    norm_grad(2)
     rs.finish(dw_ref)
+    norm_grad(3)
     dk.finish(dk_ref)
-    norm_grad(1)
+    net.drain()
     for copy in saves:
         copy.wait()
-    net.drain()
-    halo1.drain()
-    halo2.drain()
 
 
 RS_NAMES = ["got_core", "s1", "got1", "s2", "got2", "s3", "got3", "tail", "got_tail"]
@@ -778,23 +827,22 @@
     ("coef", VM((8, D), F32)),
     ("cot_p", VM((ROWS, D), BF16)),
     ("cot_t", VM((D, ROWS), BF16)),
-    ("d_proj", VM((ROWS, 2 * D), BF16)),
+    ("d_proj0", VM((ROWS, 2 * CHUNK), BF16)),
+    ("d_proj1", VM((ROWS, 2 * CHUNK), BF16)),
     ("part", VM((2, 3, 4, 4, 4, 48, 128), BF16)),
     ("h_out1", VM((CHUNKS, 2, UTT, HALO, CHUNK), BF16)),
     ("h_got1", VM((CHUNKS, 2, UTT, HALO, CHUNK), BF16)),
     ("h_out2", VM((CHUNKS, 2, UTT, HALO, CHUNK), BF16)),
     ("h_got2", VM((CHUNKS, 2, UTT, HALO, CHUNK), BF16)),
-    ("cur1", VM((4, 2, D), F32)),
-    ("ar1", VM((10, 2, D), F32)),
-    ("cur2", VM((4, 2, D), F32)),
-    ("ar2", VM((10, 2, D), F32)),
+    ("cur", VM((4, 4, 2, HALF), F32)),
+    ("got", VM((4, 10, 2, HALF), F32)),
     ("dk_src", VM((2, 4, 8, HALF), F32)),
 ]
 SCRATCH += list(zip(RS_NAMES, RS_SCRATCH)) + list(zip(DK_NAMES, DK_SCRATCH))
 SCRATCH += [
-    ("local_sem", pltpu.SemaphoreType.DMA((8,))),
-    ("send_sem", pltpu.SemaphoreType.DMA((72,))),
-    ("recv_sem", pltpu.SemaphoreType.DMA((72,))),
+    ("local_sem", pltpu.SemaphoreType.DMA((12,))),
+    ("send_sem", pltpu.SemaphoreType.DMA((88,))),
+    ("recv_sem", pltpu.SemaphoreType.DMA((88,))),
     ("h_send1", pltpu.SemaphoreType.DMA((CHUNKS, 2))),
     ("h_recv1", pltpu.SemaphoreType.DMA((CHUNKS, 2))),
     ("h_send2", pltpu.SemaphoreType.DMA((CHUNKS, 2))),

time: 106 us -> 89.6 us (0.85)
  Pallas kernels: 104 us -> 88.2 us
    pallas_call x1, Pallas kernels: 99.3 us -> 83.4 us  [on_device(): pl.pallas_call(functools.partial(whole_kernel, lax.axis_size('seq')), out...]
where the time goes in v4:
time: 89.6 us; the launch traced here: 88.9 us
  Pallas kernels  88.2 us (98%)
    pallas_call x1, Pallas kernels, on_device(): pl.pallas_call(functools.partial(whole_kernel, lax.axis_size('seq')), out...  83.4 us
    pallas_call x1, Pallas kernels, on_device(): pl.pallas_call(finish_kernel, grid=(UTT, 2), out_shape=(full, full, jax.S...  4.82 us

profile of v4, /device:TPU:1, one launch (start us, length us, event | category | flops | bytes accessed | tf_op | source)
XLA Modules:
  0.0 88.9 jit_solution(5759328843012201229)
XLA Ops:
  0.6 83.4 %shard_map.127 = (bf16[512,1536]{1,0:T(8,128)(2,1)}, bf16[512,1536]{1,0:T(8,128)(2,1)}, f32[12,1536]{1,0:T(8,128)}, f32[32,1536]{1,0:T(8,128)}, f32[2,1536]{1,0:T(2,128)}) custom-call(bf16[2,256,1536]{2,1,0:T(8,128)(2,1)} %x_hbm.1, f32[1536]{0:T(1024)} %lng_ref.1, bf16[1536,3072]{1,0:T(8,128)(2,1)} %win_hbm.1, f32[32,1536]{1,0:T(8,128)} %ker_ref.1, ...), custom_call_target="tpu_custom_call" | custom-call | tf_op jit(solution)/shard_map/pallas_call | solution.py:872
  84.1 4.8 %shard_map.128 = (bf16[2,256,1536]{2,1,0:T(8,128)(2,1)}, bf16[2,256,1536]{2,1,0:T(8,128)(2,1)}, f32[12,1536]{1,0:T(8,128)}, f32[32,1536]{1,0:T(8,128)}, f32[1536]{0:T(1024)}, /*index=5*/f32[1536]{0:T(1024)}) custom-call(bf16[512,1536]{1,0:T(8,128)(2,1)} %get-tuple-element.11.out_p, bf16[512,1536]{1,0:T(8,128)(2,1)} %get-tuple-element.12.din_p, ...), custom_call_target="tpu_custom_call" | custom-call | tf_op jit(solution)/shard_map/pallas_call | solution.py:896

commit v5 on v4

--- a/solution.py
+++ b/solution.py
@@ -427,7 +427,7 @@
             )
         return found
 
-    for copy in load_x + load_in(0):
+    for copy in load_x:
         copy.start()
     vec = s["vec"]
     for row, ref in enumerate((lng_ref, bng_ref, bnb_ref)):
@@ -451,7 +451,7 @@
     x_p, normed, mu_ref, rstd_ref = s["x_p"], s["bf"], s["mu"], s["rstd"]
     for copy in load_x:
         copy.wait()
-    for c in range(1, CHUNKS):
+    for c in range(CHUNKS):
         for copy in load_in(c):
             copy.start()
 
@@ -461,7 +461,7 @@
             x_p[u * 256 : u * 256 + 256, cols] = dot(perm[...], s["x_raw"][u, :, cols]).astype(BF16)
         return carry
 
-    lax.fori_loop(0, CHUNKS, permute, 0)
+    lax.fori_loop(0, CHUNKS, permute, 0, unroll=2)
 
     def norm_tile(i, carry):
         rows = span(i, 16)
@@ -629,7 +629,7 @@
 
     def use_sums(h):
         sums = ar2[h].take()
-        dbn_ref[:, wide[h]] = sums
+        s["dbn_s"][:, wide[h]] = sums
         gain_row = vec[1:2, wide[h]]
         rstd_row = coef[1:2, wide[h]]
         coef[2:3, wide[h]] = rstd_row * gain_row
@@ -651,10 +651,10 @@
     weight_part(1, 1)
     ar2[1].step()
     weight_part(1, 2)
+    firsts = {p: rs.start(p) for p in (2, 1, 0)}
     lax.fori_loop(0, CHUNKS // 2, branch, 0)
     ar2[0].step()
     ar2[1].step()
-    firsts = [rs.start(p) for p in range(3)]
     lax.fori_loop(CHUNKS // 2, CHUNKS, branch, 0)
     copy = pltpu.make_async_copy(s["out_p"], out_hbm, local.at[4])
     copy.start()
@@ -669,7 +669,6 @@
             xhat = conv[u * 256 : u * 256 + 256, cols]
             d_conv = d_bn * coef[2:3, cols] - coef[3:4, cols] - xhat * coef[4:5, cols]
             ext_d[u, OWN : OWN + 256, cols] = d_conv
-            conv[u * 256 : u * 256 + 256, cols] = jnp.zeros((256, CHUNK), F32)
             blocks.append(d_conv.astype(BF16))
         halo2.push(c, select, blocks)
         return carry
@@ -698,14 +697,13 @@
 
     lax.fori_loop(0, 3, conv_grad, 0)
     ar2[1].step()
+    levels = {}
+    for p in (2, 1, 0):
+        rs.add_core(p, firsts[p])
+        levels[p] = rs.send_level(p, 0)
     kernel_grad(0)
     use_sums(1)
     lax.fori_loop(3, CHUNKS, conv_grad, 0)
-
-    levels = []
-    for p in range(3):
-        rs.add_core(p, firsts[p])
-        levels.append(rs.send_level(p, 0))
 
     dk = DKernel(net, dk_src, *[s[name] for name in DK_NAMES])
     kernel_grad(1)
@@ -738,38 +736,47 @@
         for n in range(CHUNKS):
             rows = slice(n * CHUNK, n * CHUNK + CHUNK)
             weights = jnp.concatenate([w_in[rows, cols], w_in[rows, gate_cols]], axis=1)
-            conv[:, rows] += dot_t(d_proj[...], weights)
-
-    def both(j, carry):
-        for odd in range(2):
-            c = 2 * j + odd
-            input_grad(c + 1, grads[1 - odd])
-            frame_grad(c, grads[odd])
-        return carry
+            if c == 0:
+                conv[:, rows] = dot_t(d_proj[...], weights)
+            else:
+                conv[:, rows] += dot_t(d_proj[...], weights)
+
+    def pair(c):
+        input_grad(c + 1, grads[1 - c % 2])
+        frame_grad(c, grads[c % 2])
+
+    def next_level(level):
+        found = {}
+        for p in (2, 1, 0):
+            rs.add_level(p, level, levels[p])
+            found[p] = rs.send_level(p, level + 1)
+        return found
 
     input_grad(0, grads[0])
-    lax.fori_loop(0, 1, both, 0)
+    pair(0)
     dk.to_x()
-    nexts = []
-    for p in range(3):
-        rs.add_level(p, 0, levels[p])
-        nexts.append(rs.send_level(p, 1))
-    lax.fori_loop(1, 2, both, 0)
+    pair(1)
     dk.to_z()
-    levels = nexts
-    nexts = []
-    for p in range(3):
-        rs.add_level(p, 1, levels[p])
-        nexts.append(rs.send_level(p, 2))
+    levels = next_level(0)
+    pair(2)
+    dk.to_y()
+    pair(3)
+    dk.gather_x()
+    levels = next_level(1)
     input_grad(5, grads[1])
-    dk.to_y()
-    frame_grad(4, grads[0])
     halo1.drain()
     halo2.drain()
-    rs.exchange([rs.add_level(p, 2, nexts[p]) for p in range(3)])
-    dk.gather_x()
+    dk.gather_core()
+    frame_grad(4, grads[0])
     frame_grad(5, grads[1])
-    dk.gather_core()
+    rs.exchange([rs.add_level(p, 2, levels[p]) for p in range(3)])
+
+    def leave(src, dst, sem):
+        copy = pltpu.make_async_copy(src, dst, local.at[sem])
+        copy.start()
+        saves.append(copy)
+
+    leave(s["dbn_s"], dbn_ref, 10)
 
     def norm_grad(u):
         def tile(i, carry):
@@ -791,10 +798,12 @@
 
     norm_grad(0)
     norm_grad(1)
+    dk.finish(s["dk_s"])
+    leave(s["dk_s"], dk_ref, 11)
     norm_grad(2)
-    rs.finish(dw_ref)
+    rs.finish(s["dw_s"])
+    leave(s["dw_s"], dw_ref, 5)
     norm_grad(3)
-    dk.finish(dk_ref)
     net.drain()
     for copy in saves:
         copy.wait()
@@ -823,6 +832,9 @@
     ("ext_g", VM((UTT, 512, D), F32)),
     ("ext_d", VM((UTT, 512, D), F32)),
     ("conv", VM((ROWS, D), F32)),
+    ("dbn_s", VM((2, D), F32)),
+    ("dk_s", VM((K, D), F32)),
+    ("dw_s", VM((D // 128, D), F32)),
     ("stat", VM((2, D), F32)),
     ("coef", VM((8, D), F32)),
     ("cot_p", VM((ROWS, D), BF16)),
@@ -879,7 +891,7 @@
             jax.ShapeDtypeStruct((2, D), F32),
         ),
         in_specs=[any_spec, vmem_spec, any_spec, vmem_spec, vmem_spec, vmem_spec, any_spec, any_spec],
-        out_specs=[any_spec, any_spec, vmem_spec, vmem_spec, vmem_spec],
+        out_specs=[any_spec] * 5,
         scratch_shapes=[spec for _, spec in SCRATCH],
         compiler_params=pltpu.CompilerParams(
             collective_id=0, has_side_effects=True, vmem_limit_bytes=67043328

time: 89.6 us -> 86.9 us (0.970)
  Pallas kernels: 88.2 us -> 86 us
    pallas_call x1, Pallas kernels: 83.4 us -> 81.2 us  [on_device(): pl.pallas_call(functools.partial(whole_kernel, lax.axis_size('seq')), out...]
where the time goes in v5:
time: 86.9 us; the launch traced here: 86.7 us
  Pallas kernels  86 us (99%)
    pallas_call x1, Pallas kernels, on_device(): pl.pallas_call(functools.partial(whole_kernel, lax.axis_size('seq')), out...  81.2 us
    pallas_call x1, Pallas kernels, on_device(): pl.pallas_call(finish_kernel, grid=(UTT, 2), out_shape=(full, full, jax.S...  4.82 us

profile of v5, /device:TPU:1, one launch (start us, length us, event | category | flops | bytes accessed | tf_op | source)
XLA Modules:
  0.0 86.7 jit_solution(3843693040368246449)
XLA Ops:
  0.6 81.2 %shard_map.127 = (bf16[512,1536]{1,0:T(8,128)(2,1)}, bf16[512,1536]{1,0:T(8,128)(2,1)}, f32[12,1536]{1,0:T(8,128)}, f32[32,1536]{1,0:T(8,128)}, f32[2,1536]{1,0:T(2,128)}) custom-call(bf16[2,256,1536]{2,1,0:T(8,128)(2,1)} %x_hbm.1, f32[1536]{0:T(1024)} %lng_ref.1, bf16[1536,3072]{1,0:T(8,128)(2,1)} %win_hbm.1, f32[32,1536]{1,0:T(8,128)} %ker_ref.1, ...), custom_call_target="tpu_custom_call" | custom-call | tf_op jit(solution)/shard_map/pallas_call | solution.py:884
  81.8 4.8 %shard_map.128 = (bf16[2,256,1536]{2,1,0:T(8,128)(2,1)}, bf16[2,256,1536]{2,1,0:T(8,128)(2,1)}, f32[12,1536]{1,0:T(8,128)}, f32[32,1536]{1,0:T(8,128)}, f32[1536]{0:T(1024)}, /*index=5*/f32[1536]{0:T(1024)}) custom-call(bf16[512,1536]{1,0:T(8,128)(2,1)} %get-tuple-element.11.out_p, bf16[512,1536]{1,0:T(8,128)(2,1)} %get-tuple-element.12.din_p, ...), custom_call_target="tpu_custom_call" | custom-call | tf_op jit(solution)/shard_map/pallas_call | solution.py:908

commit v6 on v5

--- a/solution.py
+++ b/solution.py
@@ -87,23 +87,24 @@
 
 
 class DKernel:
-    def __init__(self, net, src, core_buf, got_core, got_x, cz, got_z, cy, got_y, full, other):
+    def __init__(self, net, src, sent, core_buf, got_core, got_x, cz, got_z, cy, got_y, full, other):
         self.net = net
-        self.src, self.core_buf, self.got_core = src, core_buf, got_core
+        self.src, self.sent, self.core_buf, self.got_core = src, sent, core_buf, got_core
         self.got_x, self.cz, self.got_z = got_x, cz, got_z
         self.cy, self.got_y, self.full, self.other = cy, got_y, full, other
 
     def start(self):
         me = self.net.me
         core = coord(me, "core")
-        self.c0 = [self.net.send(self.src.at[1 - core], self.got_core, me + 1 - 2 * core)]
+        self.sent[...] = self.src[1 - core].astype(BF16)
+        self.c0 = [self.net.send(self.sent, self.got_core, me + 1 - 2 * core)]
 
     def to_x(self):
         me = self.net.me
         core = coord(me, "core")
         x = coord(me, "x")
         self.c0[0].wait_recv()
-        self.core_buf[...] = self.src[core] + self.got_core[...]
+        self.core_buf[...] = (self.src[core] + self.got_core[...].astype(F32)).astype(BF16)
         self.cx_c = [
             self.net.send(self.core_buf.at[other], self.got_x.at[i], device)
             for i, (other, device) in enumerate(peers(me, "x"))
@@ -111,11 +112,11 @@
 
     def to_z(self):
         me = self.net.me
-        total = self.core_buf[coord(me, "x")]
+        total = self.core_buf[coord(me, "x")].astype(F32)
         for i, copy in enumerate(self.cx_c):
             copy.wait_recv()
-            total = total + self.got_x[i]
-        self.cz[...] = total
+            total = total + self.got_x[i].astype(F32)
+        self.cz[...] = total.astype(BF16)
         self.cz_c = [
             self.net.send(self.cz, self.got_z.at[i], device)
             for i, (_, device) in enumerate(peers(me, "z"))
@@ -123,11 +124,11 @@
 
     def to_y(self):
         me = self.net.me
-        total = self.cz[...]
+        total = self.cz[...].astype(F32)
         for i, copy in enumerate(self.cz_c):
             copy.wait_recv()
-            total = total + self.got_z[i]
-        self.cy[...] = total
+            total = total + self.got_z[i].astype(F32)
+        self.cy[...] = total.astype(BF16)
         self.cy_c = [
             self.net.send(self.cy, self.got_y.at[i], device)
             for i, (_, device) in enumerate(peers(me, "y"))
@@ -135,12 +136,12 @@
 
     def gather_x(self):
         me = self.net.me
-        total = self.cy[...]
+        total = self.cy[...].astype(F32)
         for i, copy in enumerate(self.cy_c):
             copy.wait_recv()
-            total = total + self.got_y[i]
+            total = total + self.got_y[i].astype(F32)
         x = coord(me, "x")
-        self.full[x] = total
+        self.full[x] = total.astype(BF16)
         self.gx_c = [
             self.net.send(self.full.at[x], self.full.at[x], device)
             for _, device in peers(me, "x")
@@ -157,22 +158,23 @@
         core = coord(self.net.me, "core")
         self.gc_c.wait_recv()
         for i in range(4):
-            mine = self.full[i]
-            theirs = self.other[i]
+            mine = self.full[i].astype(F32)
+            theirs = self.other[i].astype(F32)
             out[pl.ds(8 * i, 8), 0:HALF] = jnp.where(core == 0, mine, theirs)
             out[pl.ds(8 * i, 8), HALF:D] = jnp.where(core == 0, theirs, mine)
 
 
 DK_SCRATCH = [
-    pltpu.VMEM((4, 8, HALF), F32),
-    pltpu.VMEM((4, 8, HALF), F32),
-    pltpu.VMEM((3, 8, HALF), F32),
-    pltpu.VMEM((8, HALF), F32),
-    pltpu.VMEM((3, 8, HALF), F32),
-    pltpu.VMEM((8, HALF), F32),
-    pltpu.VMEM((3, 8, HALF), F32),
-    pltpu.VMEM((4, 8, HALF), F32),
-    pltpu.VMEM((4, 8, HALF), F32),
+    pltpu.VMEM((4, 8, HALF), BF16),
+    pltpu.VMEM((4, 8, HALF), BF16),
+    pltpu.VMEM((4, 8, HALF), BF16),
+    pltpu.VMEM((3, 8, HALF), BF16),
+    pltpu.VMEM((8, HALF), BF16),
+    pltpu.VMEM((3, 8, HALF), BF16),
+    pltpu.VMEM((8, HALF), BF16),
+    pltpu.VMEM((3, 8, HALF), BF16),
+    pltpu.VMEM((4, 8, HALF), BF16),
+    pltpu.VMEM((4, 8, HALF), BF16),
 ]
 
 
@@ -641,16 +643,16 @@
     ar2[0].start(stat[:, wide[0]])
     weight_part(0, 0)
     weight_part(0, 1)
+    weight_part(0, 2)
     ar2[0].step()
-    weight_part(0, 2)
     use_stats(1)
     lax.fori_loop(6, 12, bn_block, 0)
     ar2[0].step()
     ar2[1].start(stat[:, wide[1]])
     weight_part(1, 0)
     weight_part(1, 1)
+    weight_part(1, 2)
     ar2[1].step()
-    weight_part(1, 2)
     firsts = {p: rs.start(p) for p in (2, 1, 0)}
     lax.fori_loop(0, CHUNKS // 2, branch, 0)
     ar2[0].step()
@@ -753,20 +755,20 @@
         return found
 
     input_grad(0, grads[0])
+    dk.to_x()
     pair(0)
-    dk.to_x()
+    dk.to_z()
     pair(1)
-    dk.to_z()
     levels = next_level(0)
+    dk.to_y()
     pair(2)
-    dk.to_y()
+    dk.gather_x()
     pair(3)
-    dk.gather_x()
+    dk.gather_core()
     levels = next_level(1)
     input_grad(5, grads[1])
     halo1.drain()
     halo2.drain()
-    dk.gather_core()
     frame_grad(4, grads[0])
     frame_grad(5, grads[1])
     rs.exchange([rs.add_level(p, 2, levels[p]) for p in range(3)])

time: 86.9 us -> 87.3 us (level)
  no operation moved by 1% of the time
where the time goes in v6:
time: 87.3 us; the launch traced here: 87.1 us
  Pallas kernels  86.5 us (99%)
    pallas_call x1, Pallas kernels, on_device(): pl.pallas_call(functools.partial(whole_kernel, lax.axis_size('seq')), out...  81.6 us
    pallas_call x1, Pallas kernels, on_device(): pl.pallas_call(finish_kernel, grid=(UTT, 2), out_shape=(full, full, jax.S...  4.82 us

profile of v6, /device:TPU:1, one launch (start us, length us, event | category | flops | bytes accessed | tf_op | source)
XLA Modules:
  0.0 87.1 jit_solution(11276440445537021750)
XLA Ops:
  0.6 81.6 %shard_map.127 = (bf16[512,1536]{1,0:T(8,128)(2,1)}, bf16[512,1536]{1,0:T(8,128)(2,1)}, f32[12,1536]{1,0:T(8,128)}, f32[32,1536]{1,0:T(8,128)}, f32[2,1536]{1,0:T(2,128)}) custom-call(bf16[2,256,1536]{2,1,0:T(8,128)(2,1)} %x_hbm.1, f32[1536]{0:T(1024)} %lng_ref.1, bf16[1536,3072]{1,0:T(8,128)(2,1)} %win_hbm.1, f32[32,1536]{1,0:T(8,128)} %ker_ref.1, ...), custom_call_target="tpu_custom_call" | custom-call | tf_op jit(solution)/shard_map/pallas_call | solution.py:886
  82.3 4.8 %shard_map.128 = (bf16[2,256,1536]{2,1,0:T(8,128)(2,1)}, bf16[2,256,1536]{2,1,0:T(8,128)(2,1)}, f32[12,1536]{1,0:T(8,128)}, f32[32,1536]{1,0:T(8,128)}, f32[1536]{0:T(1024)}, /*index=5*/f32[1536]{0:T(1024)}) custom-call(bf16[512,1536]{1,0:T(8,128)(2,1)} %get-tuple-element.11.out_p, bf16[512,1536]{1,0:T(8,128)(2,1)} %get-tuple-element.12.din_p, ...), custom_call_target="tpu_custom_call" | custom-call | tf_op jit(solution)/shard_map/pallas_call | solution.py:910

commit v7 on v6

--- a/solution.py
+++ b/solution.py
@@ -87,24 +87,23 @@
 
 
 class DKernel:
-    def __init__(self, net, src, sent, core_buf, got_core, got_x, cz, got_z, cy, got_y, full, other):
+    def __init__(self, net, src, core_buf, got_core, got_x, cz, got_z, cy, got_y, full, other):
         self.net = net
-        self.src, self.sent, self.core_buf, self.got_core = src, sent, core_buf, got_core
+        self.src, self.core_buf, self.got_core = src, core_buf, got_core
         self.got_x, self.cz, self.got_z = got_x, cz, got_z
         self.cy, self.got_y, self.full, self.other = cy, got_y, full, other
 
     def start(self):
         me = self.net.me
         core = coord(me, "core")
-        self.sent[...] = self.src[1 - core].astype(BF16)
-        self.c0 = [self.net.send(self.sent, self.got_core, me + 1 - 2 * core)]
+        self.c0 = [self.net.send(self.src.at[1 - core], self.got_core, me + 1 - 2 * core)]
 
     def to_x(self):
         me = self.net.me
         core = coord(me, "core")
         x = coord(me, "x")
         self.c0[0].wait_recv()
-        self.core_buf[...] = (self.src[core] + self.got_core[...].astype(F32)).astype(BF16)
+        self.core_buf[...] = (self.src[core] + self.got_core[...]).astype(BF16)
         self.cx_c = [
             self.net.send(self.core_buf.at[other], self.got_x.at[i], device)
             for i, (other, device) in enumerate(peers(me, "x"))
@@ -166,8 +165,7 @@
 
 DK_SCRATCH = [
     pltpu.VMEM((4, 8, HALF), BF16),
-    pltpu.VMEM((4, 8, HALF), BF16),
-    pltpu.VMEM((4, 8, HALF), BF16),
+    pltpu.VMEM((4, 8, HALF), F32),
     pltpu.VMEM((3, 8, HALF), BF16),
     pltpu.VMEM((8, HALF), BF16),
     pltpu.VMEM((3, 8, HALF), BF16),
@@ -643,16 +641,16 @@
     ar2[0].start(stat[:, wide[0]])
     weight_part(0, 0)
     weight_part(0, 1)
+    ar2[0].step()
     weight_part(0, 2)
-    ar2[0].step()
     use_stats(1)
     lax.fori_loop(6, 12, bn_block, 0)
     ar2[0].step()
     ar2[1].start(stat[:, wide[1]])
     weight_part(1, 0)
     weight_part(1, 1)
+    ar2[1].step()
     weight_part(1, 2)
-    ar2[1].step()
     firsts = {p: rs.start(p) for p in (2, 1, 0)}
     lax.fori_loop(0, CHUNKS // 2, branch, 0)
     ar2[0].step()
@@ -762,14 +760,14 @@
     levels = next_level(0)
     dk.to_y()
     pair(2)
+    pair(3)
     dk.gather_x()
-    pair(3)
-    dk.gather_core()
     levels = next_level(1)
     input_grad(5, grads[1])
     halo1.drain()
     halo2.drain()
     frame_grad(4, grads[0])
+    dk.gather_core()
     frame_grad(5, grads[1])
     rs.exchange([rs.add_level(p, 2, levels[p]) for p in range(3)])
 
@@ -800,12 +798,12 @@
 
     norm_grad(0)
     norm_grad(1)
-    dk.finish(s["dk_s"])
-    leave(s["dk_s"], dk_ref, 11)
     norm_grad(2)
     rs.finish(s["dw_s"])
     leave(s["dw_s"], dw_ref, 5)
     norm_grad(3)
+    dk.finish(s["dk_s"])
+    leave(s["dk_s"], dk_ref, 11)
     net.drain()
     for copy in saves:
         copy.wait()

time: 87.3 us -> 85.4 us (0.978)
  Pallas kernels: 86.5 us -> 84.5 us
    pallas_call x1, Pallas kernels: 81.6 us -> 79.7 us  [on_device(): pl.pallas_call(functools.partial(whole_kernel, lax.axis_size('seq')), out...]
where the time goes in v7:
time: 85.4 us; the launch traced here: 85.2 us
  Pallas kernels  84.5 us (99%)
    pallas_call x1, Pallas kernels, on_device(): pl.pallas_call(functools.partial(whole_kernel, lax.axis_size('seq')), out...  79.7 us
    pallas_call x1, Pallas kernels, on_device(): pl.pallas_call(finish_kernel, grid=(UTT, 2), out_shape=(full, full, jax.S...  4.82 us

profile of v7, /device:TPU:1, one launch (start us, length us, event | category | flops | bytes accessed | tf_op | source)
XLA Modules:
  0.0 85.2 jit_solution(16679315472718015645)
XLA Ops:
  0.6 79.7 %shard_map.127 = (bf16[512,1536]{1,0:T(8,128)(2,1)}, bf16[512,1536]{1,0:T(8,128)(2,1)}, f32[12,1536]{1,0:T(8,128)}, f32[32,1536]{1,0:T(8,128)}, f32[2,1536]{1,0:T(2,128)}) custom-call(bf16[2,256,1536]{2,1,0:T(8,128)(2,1)} %x_hbm.1, f32[1536]{0:T(1024)} %lng_ref.1, bf16[1536,3072]{1,0:T(8,128)(2,1)} %win_hbm.1, f32[32,1536]{1,0:T(8,128)} %ker_ref.1, ...), custom_call_target="tpu_custom_call" | custom-call | tf_op jit(solution)/shard_map/pallas_call | solution.py:884
  80.3 4.8 %shard_map.128 = (bf16[2,256,1536]{2,1,0:T(8,128)(2,1)}, bf16[2,256,1536]{2,1,0:T(8,128)(2,1)}, f32[12,1536]{1,0:T(8,128)}, f32[32,1536]{1,0:T(8,128)}, f32[1536]{0:T(1024)}, /*index=5*/f32[1536]{0:T(1024)}) custom-call(bf16[512,1536]{1,0:T(8,128)(2,1)} %get-tuple-element.11.out_p, bf16[512,1536]{1,0:T(8,128)(2,1)} %get-tuple-element.12.din_p, ...), custom_call_target="tpu_custom_call" | custom-call | tf_op jit(solution)/shard_map/pallas_call | solution.py:908
